TPU v7x, 512 devices: a whole 4x4x16 slice. The times are simulated.
512 devices in a mesh: space: 128 (over z, y_lo, x), filt: 4 (over y_hi, core).
Axes of the slice: x: 4, y: 4 (y_hi: 2, y_lo: 2; y = y_hi * 2 + y_lo), z: 16, core: 2. Of those that a mesh axis runs over, the one named last changes fastest.
Arguments:
- inputs: bfloat16 [128, 32, 32, 256], P('space'), may hold values from -24 to 24
- out_grad: bfloat16 [128, 256, 1024], P('space', 'filt'), may hold values from -6 to 6
- pre_act: bfloat16 [128, 256, 1024], P('space', 'filt'), may hold values from -8 to 8
- weight: bfloat16 [27, 256, 256], P(None, 'filt'), may hold values from -0.078125 to 0.078125
Outputs:
- grad_input: bfloat16 [128, 32, 32, 256], P('space', 'filt')
- grad_weight: float32 [256, 27, 256], P('space', None, 'filt')
All inputs are finite; a program needn't handle non-finite values.
Results may differ from a plain program's by a relative error of at most 0.0049.
Values may be sent and summed in bfloat16 or wider, within the bound.
A program may use at most 64 MiB of HBM per device.

v0:
```python
import jax
import jax.numpy as jnp
from jax import lax
from jax.sharding import PartitionSpec as P


def extended(block, sides, width):
    for axis, dim in sides:
        count = lax.axis_size(axis)
        forward = [(i, i + 1) for i in range(count - 1)]
        backward = [(target, source) for source, target in forward]
        low = lax.ppermute(
            lax.slice_in_dim(block, block.shape[dim] - width, None, axis=dim), axis, forward
        )
        high = lax.ppermute(lax.slice_in_dim(block, 0, width, axis=dim), axis, backward)
        block = jnp.concatenate([low, block, high], axis=dim)
    return block


def silu_grad(values):
    sig = jax.nn.sigmoid(values)
    return sig * (1.0 + values * (1.0 - sig))


def on_device(inputs, out_grad, pre_act, weight):
    slab_depth, grid_height, grid_width, in_chans = inputs.shape
    tap_count = weight.shape[0]
    filt_local = weight.shape[1]
    cell_count = slab_depth * grid_height * grid_width
    d_pre = (out_grad.astype(jnp.float32) * silu_grad(pre_act.astype(jnp.float32))).astype(
        jnp.bfloat16
    )
    rimmed = extended(d_pre, (("space", 0),), 1)
    rim_grid = rimmed.reshape(slab_depth + 2, filt_local, grid_height, grid_width)
    padded = jnp.pad(rim_grid, ((0, 0), (0, 0), (1, 1), (1, 1)))
    slices = []
    for offset_d in range(3):
        for offset_h in range(3):
            for offset_w in range(3):
                window = padded[
                    2 - offset_d : 2 - offset_d + slab_depth,
                    :,
                    2 - offset_h : 2 - offset_h + grid_height,
                    2 - offset_w : 2 - offset_w + grid_width,
                ]
                slices.append(jnp.moveaxis(window, 1, 0).reshape(filt_local, cell_count))
    stacked = jnp.concatenate(slices, axis=0)
    flat_kernel = weight.reshape(tap_count * filt_local, in_chans)
    partial_sum = lax.dot_general(
        stacked, flat_kernel, (((0,), (0,)), ((), ())), preferred_element_type=jnp.float32
    )
    in_rimmed = extended(inputs, (("space", 0),), 1)
    in_padded = jnp.pad(in_rimmed, ((0, 0), (1, 1), (1, 1), (0, 0)))
    grad_flat = jnp.moveaxis(d_pre, 1, 0).reshape(filt_local, cell_count)
    results = []
    for offset_d in range(3):
        for offset_h in range(3):
            for offset_w in range(3):
                shifted = in_padded[
                    offset_d : offset_d + slab_depth,
                    offset_h : offset_h + grid_height,
                    offset_w : offset_w + grid_width,
                ].reshape(cell_count, in_chans)
                results.append(
                    lax.dot_general(
                        shifted,
                        grad_flat,
                        (((0,), (1,)), ((), ())),
                        preferred_element_type=jnp.float32,
                    )
                )
    all_terms = jnp.stack(results, axis=1)
    grad_scale = float(cell_count * lax.axis_size("space")) ** (-0.5)
    grad_weight = lax.psum_scatter(all_terms, "space", scatter_dimension=0, tiled=True) * grad_scale
    partial_grid = partial_sum.reshape(slab_depth, grid_height, grid_width, in_chans)
    grad_input = lax.psum_scatter(partial_grid, "filt", scatter_dimension=1, tiled=True).astype(
        jnp.bfloat16
    )
    return (grad_input, grad_weight)


def solution(mesh):
    placed = (
        P("space", None, None, None),
        P("space", "filt", None),
        P("space", "filt", None),
        P(None, "filt", None),
    )
    return jax.shard_map(
        on_device,
        mesh=mesh,
        in_specs=placed,
        out_specs=(P("space", "filt", None, None), P("space", None, "filt")),
        check_vma=False,
    )
```

profile of v0, /device:TPU:16, one launch (start us, length us, event | category | flops | bytes accessed | tf_op | source)
XLA Modules:
  0.0 800.9 jit_solution(862794963913416477)
XLA Ops:
  7.2 1.2 fusion.39
  8.4 3.4 collective-permute-start
  11.8 1.3 collective-permute-start.1
  13.1 4.6 collective-permute-start.2
  17.7 1.3 collective-permute-start.3
  20.7 2.7 pad_slice_fusion
  23.4 1.3 pad_slice_fusion.1
  24.7 1.7 copy.45
  26.4 1.1 copy.44
  28.1 1.7 copy.46
  29.8 1.7 copy.47
  31.6 1.7 copy.48
  33.3 1.8 copy.49
  35.1 1.8 copy.50
  36.8 1.8 copy.51
  38.6 1.8 copy.52
  40.4 1.7 copy.53
  42.1 1.7 copy.54
  43.8 1.1 copy.55
  44.9 1.6 constant_dynamic-update-slice_fusion.22
  46.5 1.6 constant_dynamic-update-slice_fusion.21
  48.1 1.6 constant_dynamic-update-slice_fusion.20
  49.6 1.6 bitcast_dynamic-update-slice_fusion.2
  51.2 1.6 constant_dynamic-update-slice_fusion.19
  52.8 1.6 constant_dynamic-update-slice_fusion.18
  54.3 1.6 constant_dynamic-update-slice_fusion.17
  55.9 1.6 constant_dynamic-update-slice_fusion.16
  57.5 1.6 constant_dynamic-update-slice_fusion.15
  59.0 1.6 constant_dynamic-update-slice_fusion.14
  60.6 1.6 constant_dynamic-update-slice_fusion.13
  63.5 1.7 copy.56
  65.3 1.7 copy.57
  67.0 1.7 copy.58
  69.3 1.1 copy.63
  70.3 1.1 copy.64
  71.4 1.1 copy.65
  72.5 1.1 copy.66
  73.6 1.6 constant_dynamic-update-slice_fusion.11
  75.1 1.6 constant_dynamic-update-slice_fusion.10
  76.7 1.6 constant_dynamic-update-slice_fusion.9
  85.1 5.8 copy.68
  90.9 4.2 convolution_bitcast_fusion
  95.4 1.1 select_maximum_fusion
  96.9 2.5 fusion.67
  100.3 0.8 fusion.28
  101.9 0.8 fusion.26
  102.8 0.8 fusion.32
  103.6 0.8 fusion.25
  106.1 0.8 fusion.22
  107.8 0.8 fusion.20
  109.5 0.8 fusion.18
  110.3 0.8 fusion.31
  112.0 0.8 fusion.16
  112.8 0.8 fusion.15
  113.6 0.9 fusion.14
  116.2 0.8 fusion.11
  117.0 0.8 fusion.10
  119.5 0.8 fusion.8
  120.3 0.8 fusion.7
  121.2 0.8 fusion.6
  122.0 5.5 copy.69
  127.6 23.6 %reduce-scatter.3.cloned.1.call-done = f32[1,8,32,256]{3,2,1,0:T(8,128)} async-done(((f32[1,32,32,256]{3,2,1,0:T(8,128)}), f32[1,8,32,256]{3,2,1,0:T(8,128)}) %reduce-scatter.3.cloned.1.call-update) | async-done | bytes 262160 | tf_op jit(solution)/shard_map/reduce_scatter | solution.py:76
  151.2 1.6 convert_element_type.19
  152.8 639.9 %reduce-scatter.5.cloned.1.call-done = f32[2,27,64]{2,1,0:T(8,128)} async-done(((f32[256,27,64]{2,1,0:T(8,128)}), f32[2,27,64]{2,1,0:T(8,128)}) %reduce-scatter.5.cloned.1.call-update) | async-done | bytes 13840 | tf_op jit(solution)/shard_map/reduce_scatter | solution.py:74
  (58 shorter events, 22.3 us)
Async XLA Ops:
  7.2 83.7 %copy-start = (bf16[27,64,256]{2,1,0:T(8,128)(2,1)S(1)}, bf16[27,64,256]{2,1,0:T(8,128)(2,1)}, u32[]{:S(2)}) copy-start(bf16[27,64,256]{2,1,0:T(8,128)(2,1)} %param.7) | copy-start | bytes 2654212
  7.2 144.0 %reduce-scatter.3.cloned.1.call-start = ((), (), s32[]{:S(2)}) async-start(), calls=%async_computation.2 | async-start | bytes 1310720 | tf_op jit(solution)/shard_map/reduce_scatter | solution.py:76
  8.4 10.6 %collective-permute-start = (bf16[1,64,1024]{2,1,0:T(8,128)(2,1)S(1)}, bf16[1,64,1024]{2,1,0:T(8,128)(2,1)S(1)}, u32[]{:S(2)}, u32[]{:S(2)}) collective-permute-start(bf16[1,64,1024]{2,1,0:T(8,128)(2,1)S(1)} %fusion.39), channel_id=1, source_target_pairs={{0,4},{4,8},{8,12},{12,16},{16,20},{20,24},{24,28},{28,32},{32,36}... | collective-permute-start | bytes 393224 | tf_op jit(solution)/shard_map/ppermute | solution.py:12
  11.8 7.2 collective-permute-start.1
  13.1 82.3 %collective-permute-start.2 = (bf16[1,32,32,256]{3,2,1,0:T(8,128)(2,1)}, bf16[1,32,32,256]{3,2,1,0:T(8,128)(2,1)S(1)}, u32[]{:S(2)}, u32[]{:S(2)}) collective-permute-start(bf16[1,32,32,256]{3,2,1,0:T(8,128)(2,1)} %param.4), channel_id=1, source_target_pairs={{0,4},{4,8},{8,12},{12,16},{16,20},{20,24},{24,28},{28,32},{32,36}... | collective-permute-start | bytes 1572872 | tf_op jit(solution)/shard_map/ppermute | solution.py:12
  17.7 77.7 %collective-permute-start.3 = (bf16[1,32,32,256]{3,2,1,0:T(8,128)(2,1)}, bf16[1,32,32,256]{3,2,1,0:T(8,128)(2,1)S(1)}, u32[]{:S(2)}, u32[]{:S(2)}) collective-permute-start(bf16[1,32,32,256]{3,2,1,0:T(8,128)(2,1)} %param.4), channel_id=1, source_target_pairs={{4,0},{8,4},{12,8},{16,12},{20,16},{24,20},{28,24},{32,28},{36,32}... | collective-permute-start | bytes 1572872 | tf_op jit(solution)/shard_map/ppermute | solution.py:15
  19.0 0.6 copy-start.5
  19.6 0.7 copy-start.7
  35.1 33.6 %copy-start.4 = (bf16[1,64,32,32]{1,3,2,0:T(8,128)(2,1)S(1)}, bf16[1,64,32,32]{1,3,2,0:T(8,128)(2,1)}, u32[]{:S(2)}) copy-start(bf16[1,64,32,32]{1,3,2,0:T(8,128)(2,1)} %get-tuple-element.51) | copy-start | bytes 393220
  36.8 32.0 %copy-start.3 = (bf16[1,64,32,32]{1,3,2,0:T(8,128)(2,1)S(1)}, bf16[1,64,32,32]{1,3,2,0:T(8,128)(2,1)}, u32[]{:S(2)}) copy-start(bf16[1,64,32,32]{1,3,2,0:T(8,128)(2,1)} %get-tuple-element.52) | copy-start | bytes 393220
  38.6 30.4 %copy-start.2 = (bf16[1,64,32,32]{1,3,2,0:T(8,128)(2,1)S(1)}, bf16[1,64,32,32]{1,3,2,0:T(8,128)(2,1)}, u32[]{:S(2)}) copy-start(bf16[1,64,32,32]{1,3,2,0:T(8,128)(2,1)} %get-tuple-element.53) | copy-start | bytes 393220
  68.8 12.8 %copy-start.6 = (bf16[1,64,1024]{2,1,0:T(8,128)(2,1)S(1)}, bf16[1,64,1024]{2,1,0:T(8,128)(2,1)}, u32[]{:S(2)}) copy-start(bf16[1,64,1024]{2,1,0:T(8,128)(2,1)} %copy-done.5) | copy-start | bytes 393220
  90.9 4.5 copy-start.1
  95.1 697.6 %reduce-scatter.5.cloned.1.call-start = ((), (), s32[]{:S(2)}) async-start(), calls=%async_computation.3 | async-start | bytes 4227072 | tf_op jit(solution)/shard_map/reduce_scatter | solution.py:74
Sparse Core Ops, SparseCore 0:
  95.3 55.8 reduce-scatter.2
  154.0 638.6 reduce-scatter.4
where the time goes:
time: 802 us; the launch traced here: 801 us
  waiting for transfers between devices  664 us (83%)
  local copies, waits for them, and re-layouts  80.8 us (10%)
  matrix products  26.8 us (3%)
  between operations  14.3 us (2%)
  starting transfers between devices  10.8 us (1%)
    reduce_scatter x1, waiting for transfers between devices, on_device(): lax.psum_scatter(all_terms, 'space', scatter_dimension=0, tiled=True)  640 us
    unnamed x43, local copies, waits for them, and re-layouts  31.9 us
    another operation x24, local copies, waits for them, and re-layouts, on_device(): slices.append(jnp.moveaxis(window, 1, 0).reshape(filt_local, cell_count))  29.7 us
    reduce_scatter x1, waiting for transfers between devices, on_device(): lax.psum_scatter(partial_grid, 'filt', scatter_dimension=1, tiled=True)  23.6 us
    dot_general x27, matrix products, on_device(): lax.dot_general(shifted, grad_flat, (((0,), (1,)), ((), ())), preferred_e...  22.6 us
  transfers between devices with their start and end apart: 6, of which 2 were waited for; matrix products, arithmetic and copies ran while one was open for 14% of the time, Pallas kernels for 0%

commit v1 on v0

v1 whole, which is shorter than its diff:
```python
import functools

import jax
import jax.numpy as jnp
from jax import lax
from jax.experimental import pallas as pl
from jax.experimental.pallas import tpu as pltpu
from jax.sharding import PartitionSpec as P

MESH = pl.DeviceIdType.MESH
F32 = jnp.float32
BF16 = jnp.bfloat16
LAYER = 8
LANES = 128


def silu_grad(values):
    sig = jax.nn.sigmoid(values)
    return sig * (1.0 + values * (1.0 - sig))


def kernel(
    sizes, x_hbm, og_hbm, pa_hbm, w_hbm, gi_hbm, gw_hbm,
    x_ref, og_ref, pa_ref, w_ref, xt_ref, buf, gi_acc,
    halo_out, halo_in, g1_out, g1_in, g2_out, g2_in,
    z_wide, z_out, z_in, c_out, c_in, y_out, y_in, gi_ref, gw_ref,
    load_sem, store_sem, halo_ssem, halo_rsem, g1_ssem, g1_rsem, g2_ssem, g2_rsem,
    z_ssem, z_rsem, f_ssem, f_rsem,
):
    n_space, layer, height, width, chans, filt = sizes
    n_z = n_space // layer
    cells = height * width
    quarter = cells // 4
    per = chans // n_space
    rows_j = per * n_z
    slots1 = g1_out.shape[2] // LANES
    slots2 = g2_out.shape[2] // LANES
    slots = slots1 + slots2
    lanes3 = 3 * filt

    space = lax.axis_index("space")
    group = lax.axis_index("filt")
    z_me, j_me = space // layer, space % layer
    y_me, core = group // 2, group % 2

    loads = [
        pltpu.make_async_copy(src, dst, load_sem.at[i])
        for i, (src, dst) in enumerate(
            ((og_hbm, og_ref), (pa_hbm, pa_ref), (x_hbm, x_ref), (w_hbm, w_ref))
        )
    ]
    for load in loads:
        load.start()

    after = (space + 1) % n_space
    before = (space + n_space - 1) % n_space
    layer_peers = [z_me * layer + (j_me + r) % layer for r in range(1, layer)]
    z_peers = [((z_me + r) % n_z) * layer + j_me for r in range(1, n_z)]
    core_peer = y_me * 2 + (1 - core)
    y_peer = (1 - y_me) * 2 + core

    barrier = pltpu.get_barrier_semaphore()
    for peer in [after, before] + layer_peers + z_peers:
        pl.semaphore_signal(barrier, inc=1, device_id={"space": peer}, device_id_type=MESH)
    for peer in (core_peer, y_peer):
        pl.semaphore_signal(barrier, inc=1, device_id={"filt": peer}, device_id_type=MESH)

    def remote(src, dst, ssem, rsem, where):
        return pltpu.make_async_remote_copy(
            src_ref=src, dst_ref=dst, send_sem=ssem, recv_sem=rsem,
            device_id=where, device_id_type=MESH,
        )

    low = lax.broadcasted_iota(jnp.int32, (cells, LANES), 1) < filt
    col = lax.broadcasted_iota(jnp.int32, (cells, LANES), 0) % width
    half = cells // 2

    def fill(a, twice):
        up = jnp.where(col == width - 1, 0.0, pltpu.roll(twice, cells - 1, 0))
        down = jnp.where(col == 0, 0.0, pltpu.roll(twice, 1, 0))
        zero = jnp.zeros((width, lanes3), BF16)
        buf[a, 0:width, :] = zero
        buf[a, width + cells : 2 * width + cells, :] = zero
        buf[a, width : width + cells, 0:LANES] = jnp.where(low, up, twice).astype(BF16)
        buf[a, width : width + cells, LANES:lanes3] = down[:, 0 : lanes3 - LANES].astype(BF16)

    loads[0].wait()
    loads[1].wait()
    d_pre = (og_ref[...].astype(F32) * silu_grad(pa_ref[...].astype(F32))).astype(BF16).astype(F32)
    twice = jnp.transpose(jnp.concatenate([d_pre, d_pre], axis=0))
    halo_out[...] = jnp.where(low[0:half], twice[0:half], twice[half:cells]).astype(BF16)
    pl.semaphore_wait(barrier, 2 + len(layer_peers) + len(z_peers) + 2)
    halos = [
        remote(halo_out, halo_in.at[0], halo_ssem.at[0], halo_rsem.at[0], {"space": before}),
        remote(halo_out, halo_in.at[1], halo_ssem.at[1], halo_rsem.at[1], {"space": after}),
    ]
    for copy in halos:
        copy.start()
    fill(1, twice)

    loads[2].wait()
    r = lax.broadcasted_iota(jnp.int32, (chans, chans), 0)
    k = lax.broadcasted_iota(jnp.int32, (chans, chans), 1)
    source = per * layer * (r % n_z) + per * (r // rows_j) + (r // n_z) % per
    pick = jnp.where(k == source, 1.0, 0.0).astype(BF16)
    xt_ref[...] = lax.dot_general(
        pick, x_ref[...], (((1,), (1,)), ((), ())), preferred_element_type=F32
    ).astype(BF16)

    def taps(a):
        return [
            jnp.dot(
                xt_ref[...], buf[a, (2 - b) * width : (2 - b) * width + cells, :],
                preferred_element_type=F32,
            ).astype(BF16)
            for b in range(3)
        ]

    def exchange(out, into, ssem, rsem):
        copies = []
        for i, peer in enumerate(layer_peers):
            j = (j_me + 1 + i) % layer
            copies.append(
                remote(out.at[j], into.at[j_me], ssem.at[i], rsem.at[j_me], {"space": peer})
            )
            copies[-1].start()
        into[j_me] = out[j_me]
        return copies

    def arrived(out, into, ssem, rsem):
        for i, peer in enumerate(layer_peers):
            j = (j_me + 1 + i) % layer
            remote(out.at[j], into.at[j], ssem.at[i], rsem.at[j], {"space": peer}).wait_recv()

    first = jnp.concatenate(taps(1) + [jnp.zeros((chans, slots1 * LANES - 9 * filt), BF16)], axis=1)
    g1_out[...] = first.reshape(layer, rows_j, slots1 * LANES)
    sends = exchange(g1_out, g1_in, g1_ssem, g1_rsem)

    def products(q, a):
        total = None
        for b in range(3):
            start = (2 - b) * width + q * quarter
            term = jnp.dot(
                buf[a, start : start + quarter, :],
                w_ref[(9 * a + 3 * b) * filt : (9 * a + 3 * b + 3) * filt, :],
                preferred_element_type=F32,
            )
            total = term if total is None else total + term
        return total

    loads[3].wait()
    for q in range(4):
        gi_acc[q] = products(q, 1)

    edges = []
    for i, a, inside in ((0, 0, space < n_space - 1), (1, 2, space > 0)):
        halos[i].wait_recv()
        packed = jnp.where(inside, halo_in[i].astype(F32), 0.0)
        turned = pltpu.roll(packed, LANES - filt, 1)
        fill(a, jnp.concatenate(
            [jnp.where(low[0:half], packed, turned), jnp.where(low[0:half], turned, packed)], axis=0
        ))
        edges += taps(a)
    g2_out[...] = jnp.concatenate(edges, axis=1).reshape(layer, rows_j, slots2 * LANES)
    sends += exchange(g2_out, g2_in, g2_ssem, g2_rsem)

    for q in range(4):
        gi_acc[q] = gi_acc[q] + products(q, 0) + products(q, 2)
    for y in range(2):
        c_out[y] = gi_acc[2 * y + (1 - core)].astype(BF16)
    cores = remote(c_out, c_in, f_ssem.at[0], f_rsem.at[0], {"filt": core_peer})
    cores.start()

    def gather(into, count, base):
        for l in range(count):
            total = into[0, :, l * LANES : (l + 1) * LANES].astype(F32)
            for j in range(1, layer):
                total = total + into[j, :, l * LANES : (l + 1) * LANES].astype(F32)
            for e in range(per):
                z_wide[:, e * slots + base + l, :] = total[e * n_z : (e + 1) * n_z]

    arrived(g1_out, g1_in, g1_ssem, g1_rsem)
    gather(g1_in, slots1, 0)

    cores.wait_recv()
    y_out[...] = (gi_acc[2 * (1 - y_me) + core] + c_in[1 - y_me].astype(F32)).astype(BF16)
    ys = remote(y_out, y_in, f_ssem.at[1], f_rsem.at[1], {"filt": y_peer})
    ys.start()

    arrived(g2_out, g2_in, g2_ssem, g2_rsem)
    gather(g2_in, slots2, slots1)
    rows = per * slots
    z_out[:, 0:rows, :] = z_wide[:, 0:rows, :].astype(BF16)
    if z_out.shape[1] > rows:
        z_out[:, rows:, :] = jnp.zeros((n_z, z_out.shape[1] - rows, LANES), BF16)
    for i, peer in enumerate(z_peers):
        z = (z_me + 1 + i) % n_z
        sends.append(remote(z_out.at[z], z_in.at[z_me], z_ssem.at[i], z_rsem.at[z_me], {"space": peer}))
        sends[-1].start()
    z_in[z_me] = z_out[z_me]

    ys.wait_recv()
    gi_ref[...] = (gi_acc[2 * y_me + core] + c_in[y_me].astype(F32) + y_in[...].astype(F32)).astype(BF16)
    store_gi = pltpu.make_async_copy(gi_ref, gi_hbm, store_sem.at[0])
    store_gi.start()

    for i, peer in enumerate(z_peers):
        z = (z_me + 1 + i) % n_z
        remote(z_out.at[z], z_in.at[z], z_ssem.at[i], z_rsem.at[z], {"space": peer}).wait_recv()
    total = z_in[0].astype(F32)
    for z in range(1, n_z):
        total = total + z_in[z].astype(F32)
    total = total * (float(cells * n_space) ** -0.5)
    for e in range(per):
        for slot in range(2 * slots):
            if slot == 9:
                continue
            tap = slot + 9 if slot < 9 else slot - 10 if slot < 19 else slot - 1
            row, part = e * slots + slot // 2, slot % 2
            gw_ref[e, tap : tap + 1, :] = total[row : row + 1, part * filt : (part + 1) * filt]
    store_gw = pltpu.make_async_copy(gw_ref, gw_hbm, store_sem.at[1])
    store_gw.start()

    for copy in halos + sends + [cores, ys]:
        copy.wait_send()
    store_gi.wait()
    store_gw.wait()


def on_device(layer, inputs, out_grad, pre_act, weight):
    _, height, width, chans = inputs.shape
    n_taps, filt, _ = weight.shape
    n_space = lax.axis_size("space")
    cells = height * width
    n_z = n_space // layer
    per = chans // n_space
    rows_j = per * n_z
    wide1 = 10 * filt
    wide2 = 18 * filt
    rows = -(-per * (wide1 + wide2) // LANES // 16) * 16
    quarter = cells // 4
    sizes = (n_space, layer, height, width, chans, filt)
    dma = pltpu.SemaphoreType.DMA
    vmem = pltpu.VMEM
    grad_input, grad_weight = pl.pallas_call(
        functools.partial(kernel, sizes),
        out_shape=(
            jax.ShapeDtypeStruct((quarter, chans), BF16),
            jax.ShapeDtypeStruct((per, n_taps, filt), F32),
        ),
        in_specs=[pl.BlockSpec(memory_space=pl.ANY)] * 4,
        out_specs=(pl.BlockSpec(memory_space=pl.ANY),) * 2,
        scratch_shapes=[
            vmem((cells, chans), BF16), vmem((filt, cells), BF16), vmem((filt, cells), BF16),
            vmem((n_taps * filt, chans), BF16), vmem((chans, cells), BF16),
            vmem((3, cells + 2 * width, 3 * filt), BF16), vmem((4, quarter, chans), F32),
            vmem((cells // 2, LANES), BF16), vmem((2, cells // 2, LANES), BF16),
            vmem((layer, rows_j, wide1), BF16), vmem((layer, rows_j, wide1), BF16),
            vmem((layer, rows_j, wide2), BF16), vmem((layer, rows_j, wide2), BF16),
            vmem((n_z, rows, LANES), F32), vmem((n_z, rows, LANES), BF16), vmem((n_z, rows, LANES), BF16),
            vmem((2, quarter, chans), BF16), vmem((2, quarter, chans), BF16),
            vmem((quarter, chans), BF16), vmem((quarter, chans), BF16),
            vmem((quarter, chans), BF16), vmem((per, n_taps, filt), F32),
            dma((4,)), dma((2,)), dma((2,)), dma((2,)),
            dma((layer - 1,)), dma((layer,)), dma((layer - 1,)), dma((layer,)),
            dma((n_z - 1,)), dma((n_z,)), dma((2,)), dma((2,)),
        ],
        compiler_params=pltpu.CompilerParams(collective_id=0, has_side_effects=True),
        name="conv_backward",
    )(
        inputs.reshape(cells, chans), out_grad.reshape(filt, cells), pre_act.reshape(filt, cells),
        weight.reshape(n_taps * filt, chans),
    )
    return grad_input.reshape(1, height // 4, width, chans), grad_weight


def solution(mesh, layer=LAYER):
    placed = (
        P("space", None, None, None),
        P("space", "filt", None),
        P("space", "filt", None),
        P(None, "filt", None),
    )
    return jax.shard_map(
        functools.partial(on_device, layer),
        mesh=mesh,
        in_specs=placed,
        out_specs=(P("space", "filt", None, None), P("space", None, "filt")),
        check_vma=False,
    )
```

time: 802 us -> 45.6 us (0.06)
  the two profiles are of different devices: /device:TPU:16 before, /device:TPU:1 now
where the time goes in v1:
time: 45.6 us; the launch traced here: 45.4 us
  Pallas kernels  41.8 us (92%)
  local copies, waits for them, and re-layouts  2.96 us (6%)
  between operations  0.64 us (1%)
    pallas_call x1, Pallas kernels, on_device(): pl.pallas_call(functools.partial(kernel, sizes), out_shape=(jax.ShapeDtyp...  41.8 us
    unnamed x2, local copies, waits for them, and re-layouts  2.96 us

profile of v1, /device:TPU:1, one launch (start us, length us, event | category | flops | bytes accessed | tf_op | source)
XLA Modules:
  0.0 45.4 jit_solution(13154290420090424004)
XLA Ops:
  0.6 41.8 %conv_backward.1 = (bf16[256,256]{1,0:T(8,128)(2,1)}, f32[2,27,64]{2,1,0:T(8,128)}) custom-call(bf16[1024,256]{1,0:T(8,128)(2,1)} %bitcast.6, bf16[64,1024]{1,0:T(8,128)(2,1)} %bitcast.7, bf16[64,1024]{1,0:T(8,128)(2,1)} %bitcast.8, bf16[1728,256]{1,0:T(8,128)(2,1)} %bitcast.5), custom_call_target="tpu_custom_call" | custom-call | tf_op jit(solution)/shard_map/conv_backward/pallas_call | solution.py:245
  42.4 1.4 %copy.6 = f32[2,27,64]{2,0,1:T(2,128)} copy(f32[2,27,64]{2,1,0:T(8,128)} %get-tuple-element.7) | data formatting | bytes 27648
  43.8 1.6 %copy.8 = bf16[1,8,32,256]{3,2,1,0:T(8,128)(2,1)} copy(bf16[1,8,32,256]{3,2,1,0:T(8,128)(2,1)} %bitcast.9) | data formatting | bytes 262144

commit v2 on v1

v2 whole, which is shorter than its diff:
```python
import functools

import jax
import jax.numpy as jnp
from jax import lax
from jax.experimental import pallas as pl
from jax.experimental.pallas import tpu as pltpu
from jax.sharding import PartitionSpec as P

MESH = pl.DeviceIdType.MESH
F32 = jnp.float32
BF16 = jnp.bfloat16
LAYER = 8
LANES = 128


def silu_grad(values):
    sig = jax.nn.sigmoid(values)
    return sig * (1.0 + values * (1.0 - sig))


def kernel(
    sizes, x_hbm, og_hbm, pa_hbm, w_hbm, gi_hbm, gw_hbm,
    x_ref, og_ref, pa_ref, w_ref, xt_ref, buf, gi_acc,
    halo_out, halo_in, g0_out, g0_in, g1_out, g1_in, g2_out, g2_in,
    z_wide, z0_out, z0_in, z1_out, z1_in, c_out, c_in, y_out, y_in, gi_ref, gw_ref,
    load_sem, store_sem, halo_ssem, halo_rsem, g_ssem, g_rsem, z_ssem, z_rsem, f_ssem, f_rsem, known,
):
    n_space, layer, height, width, chans, filt = sizes
    n_z = n_space // layer
    cells = height * width
    quarter = cells // 4
    per = chans // n_space
    rows_j = per * n_z
    counts = [g.shape[2] // LANES for g in (g0_out, g1_out, g2_out)]
    lanes3 = 3 * filt

    space = lax.axis_index("space")
    group = lax.axis_index("filt")
    z_me, j_me = space // layer, space % layer
    y_me, core = group // 2, group % 2

    loads = [
        pltpu.make_async_copy(src, dst, load_sem.at[i])
        for i, (src, dst) in enumerate(
            ((og_hbm, og_ref), (pa_hbm, pa_ref), (x_hbm, x_ref), (w_hbm, w_ref))
        )
    ]
    for load in loads:
        load.start()

    after = (space + 1) % n_space
    before = (space + n_space - 1) % n_space
    layer_peers = [z_me * layer + (j_me + r) % layer for r in range(1, layer)]
    far_first = sorted(range(1, n_z), key=lambda r: -min(r, n_z - r))
    core_peer = y_me * 2 + (1 - core)
    y_peer = (1 - y_me) * 2 + core

    barrier = pltpu.get_barrier_semaphore()
    def along_z(distance):
        return ((z_me + distance) % n_z) * layer + j_me

    near = [after, before] + layer_peers + [along_z(1), along_z(n_z - 1)]
    for peer in near:
        pl.semaphore_signal(barrier, inc=1, device_id={"space": peer}, device_id_type=MESH)
    for peer in (core_peer, y_peer):
        pl.semaphore_signal(barrier, inc=1, device_id={"filt": peer}, device_id_type=MESH)

    def remote(src, dst, ssem, rsem, where):
        return pltpu.make_async_remote_copy(
            src_ref=src, dst_ref=dst, send_sem=ssem, recv_sem=rsem,
            device_id=where, device_id_type=MESH,
        )

    reaches = [1 << i for i in range(n_z.bit_length()) if (1 << i) < n_z // 2]

    def tell(i):
        if i < len(reaches):
            for distance in (reaches[i], n_z - reaches[i]):
                pl.semaphore_signal(
                    known.at[i], inc=1, device_id={"space": along_z(distance)}, device_id_type=MESH
                )

    def learn(i):
        if i < len(reaches):
            pl.semaphore_wait(known.at[i], 2)

    low = lax.broadcasted_iota(jnp.int32, (cells, LANES), 1) < filt
    col = lax.broadcasted_iota(jnp.int32, (cells, LANES), 0) % width
    half = cells // 2

    def fill(a, twice):
        up = jnp.where(col == width - 1, 0.0, pltpu.roll(twice, cells - 1, 0))
        down = jnp.where(col == 0, 0.0, pltpu.roll(twice, 1, 0))
        zero = jnp.zeros((width, lanes3), BF16)
        buf[a, 0:width, :] = zero
        buf[a, width + cells : 2 * width + cells, :] = zero
        buf[a, width : width + cells, 0:LANES] = jnp.where(low, up, twice).astype(BF16)
        buf[a, width : width + cells, LANES:lanes3] = down[:, 0 : lanes3 - LANES].astype(BF16)

    loads[0].wait()
    loads[1].wait()
    d_pre = (og_ref[...].astype(F32) * silu_grad(pa_ref[...].astype(F32))).astype(BF16).astype(F32)
    twice = jnp.transpose(jnp.concatenate([d_pre, d_pre], axis=0))
    halo_out[...] = jnp.where(low[0:half], twice[0:half], twice[half:cells]).astype(BF16)
    pl.semaphore_wait(barrier, len(near) + 2)
    halos = [
        remote(halo_out, halo_in.at[0], halo_ssem.at[0], halo_rsem.at[0], {"space": before}),
        remote(halo_out, halo_in.at[1], halo_ssem.at[1], halo_rsem.at[1], {"space": after}),
    ]
    for copy in halos:
        copy.start()
    tell(0)
    fill(1, twice)

    loads[2].wait()
    r = lax.broadcasted_iota(jnp.int32, (chans, chans), 0)
    k = lax.broadcasted_iota(jnp.int32, (chans, chans), 1)
    source = per * layer * (r % n_z) + per * (r // rows_j) + (r // n_z) % per
    pick = jnp.where(k == source, 1.0, 0.0).astype(BF16)
    xt_ref[...] = lax.dot_general(
        pick, x_ref[...], (((1,), (1,)), ((), ())), preferred_element_type=F32
    ).astype(BF16)

    def taps(a):
        return [
            jnp.dot(
                xt_ref[...], buf[a, (2 - b) * width : (2 - b) * width + cells, :],
                preferred_element_type=F32,
            ).astype(BF16)
            for b in range(3)
        ]

    sends = []

    def exchange(part, out, into):
        for i, peer in enumerate(layer_peers):
            j = (j_me + 1 + i) % layer
            sends.append(remote(
                out.at[j], into.at[j_me], g_ssem.at[part, i], g_rsem.at[part, j_me], {"space": peer}
            ))
            sends[-1].start()
        into[j_me] = out[j_me]

    def arrived(part, out, into):
        for i, peer in enumerate(layer_peers):
            j = (j_me + 1 + i) % layer
            remote(
                out.at[j], into.at[j], g_ssem.at[part, i], g_rsem.at[part, j], {"space": peer}
            ).wait_recv()

    pad = jnp.zeros((chans, filt), BF16)
    g0_out[...] = jnp.concatenate(taps(1) + [pad], axis=1).reshape(g0_out.shape)
    exchange(0, g0_out, g0_in)
    learn(0)
    tell(1)

    def products(q, a):
        total = None
        for b in range(3):
            start = (2 - b) * width + q * quarter
            term = jnp.dot(
                buf[a, start : start + quarter, :],
                w_ref[(9 * a + 3 * b) * filt : (9 * a + 3 * b + 3) * filt, :],
                preferred_element_type=F32,
            )
            total = term if total is None else total + term
        return total

    loads[3].wait()
    for q in range(4):
        gi_acc[q] = products(q, 1)

    def edge(i, a, inside):
        halos[i].wait_recv()
        packed = jnp.where(inside, halo_in[i].astype(F32), 0.0)
        turned = pltpu.roll(packed, LANES - filt, 1)
        fill(a, jnp.concatenate(
            [jnp.where(low[0:half], packed, turned), jnp.where(low[0:half], turned, packed)], axis=0
        ))
        return jnp.concatenate(taps(a), axis=1)

    wide = g1_out.shape[2]
    lower = edge(0, 0, space < n_space - 1)
    g1_out[...] = lower[:, 0:wide].reshape(g1_out.shape)
    exchange(1, g1_out, g1_in)
    upper = edge(1, 2, space > 0)
    g2_out[...] = jnp.concatenate([lower[:, wide:], upper], axis=1).reshape(g2_out.shape)
    exchange(2, g2_out, g2_in)
    learn(1)
    tell(2)

    for q in range(4):
        gi_acc[q] = gi_acc[q] + products(q, 0) + products(q, 2)
    for y in range(2):
        c_out[y] = gi_acc[2 * y + (1 - core)].astype(BF16)
    cores = remote(c_out, c_in, f_ssem.at[0], f_rsem.at[0], {"filt": core_peer})
    cores.start()

    def gather(into, count, stride, base):
        for l in range(count):
            total = into[0, :, l * LANES : (l + 1) * LANES].astype(F32)
            for j in range(1, layer):
                total = total + into[j, :, l * LANES : (l + 1) * LANES].astype(F32)
            for e in range(per):
                z_wide[:, e * stride + base + l, :] = total[e * n_z : (e + 1) * n_z]

    def spread(part, out, into):
        out[...] = z_wide[:, 0 : out.shape[1], :].astype(BF16)
        for i, distance in enumerate(far_first):
            z = (z_me + distance) % n_z
            sends.append(remote(
                out.at[z], into.at[z_me], z_ssem.at[part, i], z_rsem.at[part, z_me],
                {"space": along_z(distance)},
            ))
            sends[-1].start()
        into[z_me] = out[z_me]

    def summed(part, out, into):
        for i, distance in enumerate(far_first):
            z = (z_me + distance) % n_z
            remote(
                out.at[z], into.at[z], z_ssem.at[part, i], z_rsem.at[part, z],
                {"space": along_z(distance)},
            ).wait_recv()
        total = into[0].astype(F32)
        for z in range(1, n_z):
            total = total + into[z].astype(F32)
        return total * (float(cells * n_space) ** -0.5)

    arrived(0, g0_out, g0_in)
    gather(g0_in, counts[0], counts[0], 0)
    learn(2)
    spread(0, z0_out, z0_in)

    cores.wait_recv()
    y_out[...] = (gi_acc[2 * (1 - y_me) + core] + c_in[1 - y_me].astype(F32)).astype(BF16)
    ys = remote(y_out, y_in, f_ssem.at[1], f_rsem.at[1], {"filt": y_peer})
    ys.start()

    rest = counts[1] + counts[2]
    arrived(1, g1_out, g1_in)
    gather(g1_in, counts[1], rest, 0)
    arrived(2, g2_out, g2_in)
    gather(g2_in, counts[2], rest, counts[1])
    spread(1, z1_out, z1_in)

    ys.wait_recv()
    gi_ref[...] = (gi_acc[2 * y_me + core] + c_in[y_me].astype(F32) + y_in[...].astype(F32)).astype(BF16)
    store_gi = pltpu.make_async_copy(gi_ref, gi_hbm, store_sem.at[0])
    store_gi.start()

    def place(total, stride, taps_of):
        for e in range(per):
            for slot, tap in enumerate(taps_of):
                row, part = e * stride + slot // 2, slot % 2
                gw_ref[tap, e : e + 1, :] = total[row : row + 1, part * filt : (part + 1) * filt]

    place(summed(0, z0_out, z0_in), counts[0], range(9, 18))
    place(summed(1, z1_out, z1_in), rest, [*range(0, 9), *range(18, 27)])
    store_gw = pltpu.make_async_copy(gw_ref, gw_hbm, store_sem.at[1])
    store_gw.start()

    for copy in halos + sends + [cores, ys]:
        copy.wait_send()
    store_gi.wait()
    store_gw.wait()


def on_device(layer, inputs, out_grad, pre_act, weight):
    _, height, width, chans = inputs.shape
    n_taps, filt, _ = weight.shape
    n_space = lax.axis_size("space")
    cells = height * width
    n_z = n_space // layer
    per = chans // n_space
    rows_j = per * n_z
    widths = (10 * filt, 8 * filt, 10 * filt)
    rows0 = per * widths[0] // LANES
    rows1 = per * (widths[1] + widths[2]) // LANES
    quarter = cells // 4
    sizes = (n_space, layer, height, width, chans, filt)
    dma = pltpu.SemaphoreType.DMA
    vmem = pltpu.VMEM
    grad_input, grad_weight = pl.pallas_call(
        functools.partial(kernel, sizes),
        out_shape=(
            jax.ShapeDtypeStruct((quarter, chans), BF16),
            jax.ShapeDtypeStruct((n_taps, per, filt), F32),
        ),
        in_specs=[pl.BlockSpec(memory_space=pltpu.HBM)] * 4,
        out_specs=(pl.BlockSpec(memory_space=pl.ANY),) * 2,
        scratch_shapes=[
            vmem((cells, chans), BF16), vmem((filt, cells), BF16), vmem((filt, cells), BF16),
            vmem((n_taps * filt, chans), BF16), vmem((chans, cells), BF16),
            vmem((3, cells + 2 * width, 3 * filt), BF16), vmem((4, quarter, chans), F32),
            vmem((cells // 2, LANES), BF16), vmem((2, cells // 2, LANES), BF16),
            *[vmem((layer, rows_j, widths[i // 2]), BF16) for i in range(6)],
            vmem((n_z, rows1, LANES), F32),
            vmem((n_z, rows0, LANES), BF16), vmem((n_z, rows0, LANES), BF16),
            vmem((n_z, rows1, LANES), BF16), vmem((n_z, rows1, LANES), BF16),
            vmem((2, quarter, chans), BF16), vmem((2, quarter, chans), BF16),
            vmem((quarter, chans), BF16), vmem((quarter, chans), BF16),
            vmem((quarter, chans), BF16), vmem((n_taps, per, filt), F32),
            dma((4,)), dma((2,)), dma((2,)), dma((2,)),
            dma((3, layer - 1)), dma((3, layer)), dma((2, n_z - 1)), dma((2, n_z)), dma((2,)), dma((2,)),
            pltpu.SemaphoreType.REGULAR((3,)),
        ],
        compiler_params=pltpu.CompilerParams(
            collective_id=0, has_side_effects=True, vmem_limit_bytes=24 * 1024 * 1024
        ),
        name="conv_backward",
    )(
        *[
            pltpu.with_memory_space_constraint(array, pltpu.HBM)
            for array in (
                inputs.reshape(cells, chans), out_grad.reshape(filt, cells),
                pre_act.reshape(filt, cells), weight.reshape(n_taps * filt, chans),
            )
        ]
    )
    return grad_input.reshape(1, height // 4, width, chans), jnp.swapaxes(grad_weight, 0, 1)


def solution(mesh, layer=LAYER):
    placed = (
        P("space", None, None, None),
        P("space", "filt", None),
        P("space", "filt", None),
        P(None, "filt", None),
    )
    return jax.shard_map(
        functools.partial(on_device, layer),
        mesh=mesh,
        in_specs=placed,
        out_specs=(P("space", "filt", None, None), P("space", None, "filt")),
        check_vma=False,
    )
```

time: 45.6 us -> 39.4 us (0.86)
  the two profiles are of different devices: /device:TPU:1 before, /device:TPU:16 now
where the time goes in v2:
time: 39.4 us; the launch traced here: 39.3 us
  Pallas kernels  37.4 us (95%)
  local copies, waits for them, and re-layouts  1.27 us (3%)
  between operations  0.64 us (2%)
    pallas_call x1, Pallas kernels, on_device(): pl.pallas_call(functools.partial(kernel, sizes), out_shape=(jax.ShapeDtyp...  37.4 us
    unnamed x2, local copies, waits for them, and re-layouts  1.27 us

profile of v2, /device:TPU:16, one launch (start us, length us, event | category | flops | bytes accessed | tf_op | source)
XLA Modules:
  0.0 39.3 jit_solution(4890675132478504661)
XLA Ops:
  0.6 37.4 %conv_backward.1 = (bf16[256,256]{1,0:T(8,128)(2,1)S(1)}, f32[27,2,64]{2,1,0:T(2,128)S(1)}) custom-call(bf16[1024,256]{1,0:T(8,128)(2,1)} %bitcast.9, bf16[64,1024]{1,0:T(8,128)(2,1)} %bitcast.10, bf16[64,1024]{1,0:T(8,128)(2,1)} %bitcast.11, bf16[1728,256]{1,0:T(8,128)(2,1)} %bitcast.8), custom_call_target="tpu_custom_call" | custom-call | tf_op jit(solution)/shard_map/conv_backward/pallas_call | solution.py:285
  38.0 0.7 %copy.8 = bf16[1,8,32,256]{3,2,1,0:T(8,128)(2,1)} copy(bf16[1,8,32,256]{3,2,1,0:T(8,128)(2,1)S(1)} %bitcast.6) | data formatting | bytes 262144
  38.7 0.6 %copy.9 = f32[2,27,64]{2,0,1:T(2,128)} copy(f32[2,27,64]{2,0,1:T(2,128)S(1)} %bitcast.7) | data formatting | bytes 27648

commit v3 on v2

--- a/solution.py
+++ b/solution.py
@@ -22,9 +22,9 @@
 def kernel(
     sizes, x_hbm, og_hbm, pa_hbm, w_hbm, gi_hbm, gw_hbm,
     x_ref, og_ref, pa_ref, w_ref, xt_ref, buf, gi_acc,
-    halo_out, halo_in, g0_out, g0_in, g1_out, g1_in, g2_out, g2_in,
-    z_wide, z0_out, z0_in, z1_out, z1_in, c_out, c_in, y_out, y_in, gi_ref, gw_ref,
-    load_sem, store_sem, halo_ssem, halo_rsem, g_ssem, g_rsem, z_ssem, z_rsem, f_ssem, f_rsem, known,
+    halo_out, halo_in, g_out, g_in, z_wide, m_out, m_in, e_out, e_in,
+    c_out, c_in, y_out, y_in, gi_ref, gw_ref,
+    load_sem, store_sem, halo_ssem, halo_rsem, many_ssem, many_rsem, f_ssem, f_rsem, known,
 ):
     n_space, layer, height, width, chans, filt = sizes
     n_z = n_space // layer
@@ -32,7 +32,8 @@
     quarter = cells // 4
     per = chans // n_space
     rows_j = per * n_z
-    counts = [g.shape[2] // LANES for g in (g0_out, g1_out, g2_out)]
+    tiles = g_out.shape[2]
+    full = tiles // per
     lanes3 = 3 * filt
 
     space = lax.axis_index("space")
@@ -60,7 +61,9 @@
     def along_z(distance):
         return ((z_me + distance) % n_z) * layer + j_me
 
-    near = [after, before] + layer_peers + [along_z(1), along_z(n_z - 1)]
+    reach = 1
+    near_z = sorted({d for r in range(1, reach + 1) for d in (r, n_z - r)})
+    near = [after, before] + layer_peers + [along_z(d) for d in near_z]
     for peer in near:
         pl.semaphore_signal(barrier, inc=1, device_id={"space": peer}, device_id_type=MESH)
     for peer in (core_peer, y_peer):
@@ -72,7 +75,7 @@
             device_id=where, device_id_type=MESH,
         )
 
-    reaches = [1 << i for i in range(n_z.bit_length()) if (1 << i) < n_z // 2]
+    reaches = [reach << i for i in range(n_z.bit_length()) if (reach << i) < n_z // 2]
 
     def tell(i):
         if i < len(reaches):
@@ -123,35 +126,39 @@
     ).astype(BF16)
 
     def taps(a):
-        return [
-            jnp.dot(
-                xt_ref[...], buf[a, (2 - b) * width : (2 - b) * width + cells, :],
-                preferred_element_type=F32,
-            ).astype(BF16)
-            for b in range(3)
-        ]
-
-    sends = []
-
-    def exchange(part, out, into):
-        for i, peer in enumerate(layer_peers):
-            j = (j_me + 1 + i) % layer
-            sends.append(remote(
-                out.at[j], into.at[j_me], g_ssem.at[part, i], g_rsem.at[part, j_me], {"space": peer}
-            ))
-            sends[-1].start()
-        into[j_me] = out[j_me]
-
-    def arrived(part, out, into):
-        for i, peer in enumerate(layer_peers):
-            j = (j_me + 1 + i) % layer
+        found = jnp.concatenate(
+            [
+                jnp.dot(
+                    xt_ref[...], buf[a, (2 - b) * width : (2 - b) * width + cells, :],
+                    preferred_element_type=F32,
+                ).astype(BF16)
+                for b in range(3)
+            ],
+            axis=1,
+        ).reshape(layer, per, n_z, 9 * filt)
+        for e in range(per):
+            for l in range(full):
+                g_out[a, :, e * full + l] = found[:, e, :, l * LANES : (l + 1) * LANES]
+        g_out[a, :, per * full] = jnp.concatenate(
+            [found[:, e, :, full * LANES :] for e in range(per)], axis=-1
+        )
+        exchange(a, g_out.at[a], g_in.at[a], j_me, in_layer)
+
+    in_layer = [((j_me + r) % layer, peer) for r, peer in zip(range(1, layer), layer_peers)]
+    in_column = [((z_me + d) % n_z, along_z(d)) for d in far_first]
+
+    def exchange(part, out, into, me, peers):
+        for slot, peer in peers:
             remote(
-                out.at[j], into.at[j], g_ssem.at[part, i], g_rsem.at[part, j], {"space": peer}
-            ).wait_recv()
-
-    pad = jnp.zeros((chans, filt), BF16)
-    g0_out[...] = jnp.concatenate(taps(1) + [pad], axis=1).reshape(g0_out.shape)
-    exchange(0, g0_out, g0_in)
+                out.at[slot], into.at[me], many_ssem.at[part], many_rsem.at[part], {"space": peer}
+            ).start()
+        into[me] = out[me]
+
+    def all_of(into, sem):
+        others = into.at[pl.ds(0, into.shape[0] - 1)]
+        pltpu.make_async_copy(others, others, sem).wait()
+
+    taps(1)
     learn(0)
     tell(1)
 
@@ -171,22 +178,17 @@
     for q in range(4):
         gi_acc[q] = products(q, 1)
 
-    def edge(i, a, inside):
-        halos[i].wait_recv()
+    far_next = jnp.where((j_me + 1) % (layer // 2) == 0, 1, 0)
+    for turn in range(2):
+        i = far_next if turn == 0 else 1 - far_next
+        pltpu.make_async_copy(halo_in.at[i], halo_in.at[i], halo_rsem.at[i]).wait()
+        inside = jnp.where(i == 0, n_space - 1 - space, space) > 0
         packed = jnp.where(inside, halo_in[i].astype(F32), 0.0)
         turned = pltpu.roll(packed, LANES - filt, 1)
-        fill(a, jnp.concatenate(
+        fill(2 * i, jnp.concatenate(
             [jnp.where(low[0:half], packed, turned), jnp.where(low[0:half], turned, packed)], axis=0
         ))
-        return jnp.concatenate(taps(a), axis=1)
-
-    wide = g1_out.shape[2]
-    lower = edge(0, 0, space < n_space - 1)
-    g1_out[...] = lower[:, 0:wide].reshape(g1_out.shape)
-    exchange(1, g1_out, g1_in)
-    upper = edge(1, 2, space > 0)
-    g2_out[...] = jnp.concatenate([lower[:, wide:], upper], axis=1).reshape(g2_out.shape)
-    exchange(2, g2_out, g2_in)
+        taps(2 * i)
     learn(1)
     tell(2)
 
@@ -197,71 +199,61 @@
     cores = remote(c_out, c_in, f_ssem.at[0], f_rsem.at[0], {"filt": core_peer})
     cores.start()
 
-    def gather(into, count, stride, base):
-        for l in range(count):
-            total = into[0, :, l * LANES : (l + 1) * LANES].astype(F32)
+    def gather(a, base):
+        all_of(g_in.at[a], many_rsem.at[a])
+        for t in range(tiles):
+            total = g_in[a, 0, t].astype(F32)
             for j in range(1, layer):
-                total = total + into[j, :, l * LANES : (l + 1) * LANES].astype(F32)
-            for e in range(per):
-                z_wide[:, e * stride + base + l, :] = total[e * n_z : (e + 1) * n_z]
-
-    def spread(part, out, into):
-        out[...] = z_wide[:, 0 : out.shape[1], :].astype(BF16)
-        for i, distance in enumerate(far_first):
-            z = (z_me + distance) % n_z
-            sends.append(remote(
-                out.at[z], into.at[z_me], z_ssem.at[part, i], z_rsem.at[part, z_me],
-                {"space": along_z(distance)},
-            ))
-            sends[-1].start()
-        into[z_me] = out[z_me]
-
-    def summed(part, out, into):
-        for i, distance in enumerate(far_first):
-            z = (z_me + distance) % n_z
-            remote(
-                out.at[z], into.at[z], z_ssem.at[part, i], z_rsem.at[part, z],
-                {"space": along_z(distance)},
-            ).wait_recv()
+                total = total + g_in[a, j, t].astype(F32)
+            z_wide[:, base + t, :] = total
+
+    def summed(into):
         total = into[0].astype(F32)
-        for z in range(1, n_z):
+        for z in range(1, into.shape[0]):
             total = total + into[z].astype(F32)
         return total * (float(cells * n_space) ** -0.5)
 
-    arrived(0, g0_out, g0_in)
-    gather(g0_in, counts[0], counts[0], 0)
+    def place(total, base, a):
+        for e in range(per):
+            for tap in range(9):
+                if tap < 2 * full:
+                    row, part = base + e * full + tap // 2, tap % 2
+                else:
+                    row, part = base + per * full, e
+                gw_ref[9 * a + tap, e : e + 1, :] = total[row : row + 1, part * filt : (part + 1) * filt]
+
+    gather(1, 0)
+    m_out[...] = z_wide[:, 0:tiles, :].astype(BF16)
     learn(2)
-    spread(0, z0_out, z0_in)
+    exchange(3, m_out, m_in, z_me, in_column)
 
     cores.wait_recv()
     y_out[...] = (gi_acc[2 * (1 - y_me) + core] + c_in[1 - y_me].astype(F32)).astype(BF16)
     ys = remote(y_out, y_in, f_ssem.at[1], f_rsem.at[1], {"filt": y_peer})
     ys.start()
 
-    rest = counts[1] + counts[2]
-    arrived(1, g1_out, g1_in)
-    gather(g1_in, counts[1], rest, 0)
-    arrived(2, g2_out, g2_in)
-    gather(g2_in, counts[2], rest, counts[1])
-    spread(1, z1_out, z1_in)
+    gather(0, 0)
+    gather(2, tiles)
+    e_out[...] = z_wide[...].astype(BF16)
+    exchange(4, e_out, e_in, z_me, in_column)
 
     ys.wait_recv()
     gi_ref[...] = (gi_acc[2 * y_me + core] + c_in[y_me].astype(F32) + y_in[...].astype(F32)).astype(BF16)
     store_gi = pltpu.make_async_copy(gi_ref, gi_hbm, store_sem.at[0])
     store_gi.start()
 
-    def place(total, stride, taps_of):
-        for e in range(per):
-            for slot, tap in enumerate(taps_of):
-                row, part = e * stride + slot // 2, slot % 2
-                gw_ref[tap, e : e + 1, :] = total[row : row + 1, part * filt : (part + 1) * filt]
-
-    place(summed(0, z0_out, z0_in), counts[0], range(9, 18))
-    place(summed(1, z1_out, z1_in), rest, [*range(0, 9), *range(18, 27)])
+    all_of(m_in, many_rsem.at[3])
+    place(summed(m_in), 0, 1)
+    all_of(e_in, many_rsem.at[4])
+    total = summed(e_in)
+    place(total, 0, 0)
+    place(total, tiles, 2)
     store_gw = pltpu.make_async_copy(gw_ref, gw_hbm, store_sem.at[1])
     store_gw.start()
 
-    for copy in halos + sends + [cores, ys]:
+    for part, out in enumerate((g_out.at[0], g_out.at[1], g_out.at[2], m_out, e_out)):
+        all_of(out, many_ssem.at[part])
+    for copy in halos + [cores, ys]:
         copy.wait_send()
     store_gi.wait()
     store_gw.wait()
@@ -274,10 +266,7 @@
     cells = height * width
     n_z = n_space // layer
     per = chans // n_space
-    rows_j = per * n_z
-    widths = (10 * filt, 8 * filt, 10 * filt)
-    rows0 = per * widths[0] // LANES
-    rows1 = per * (widths[1] + widths[2]) // LANES
+    tiles = per * 9 * filt // LANES
     quarter = cells // 4
     sizes = (n_space, layer, height, width, chans, filt)
     dma = pltpu.SemaphoreType.DMA
@@ -295,16 +284,15 @@
             vmem((n_taps * filt, chans), BF16), vmem((chans, cells), BF16),
             vmem((3, cells + 2 * width, 3 * filt), BF16), vmem((4, quarter, chans), F32),
             vmem((cells // 2, LANES), BF16), vmem((2, cells // 2, LANES), BF16),
-            *[vmem((layer, rows_j, widths[i // 2]), BF16) for i in range(6)],
-            vmem((n_z, rows1, LANES), F32),
-            vmem((n_z, rows0, LANES), BF16), vmem((n_z, rows0, LANES), BF16),
-            vmem((n_z, rows1, LANES), BF16), vmem((n_z, rows1, LANES), BF16),
+            vmem((3, layer, tiles, n_z, LANES), BF16), vmem((3, layer, tiles, n_z, LANES), BF16),
+            vmem((n_z, 2 * tiles, LANES), F32),
+            vmem((n_z, tiles, LANES), BF16), vmem((n_z, tiles, LANES), BF16),
+            vmem((n_z, 2 * tiles, LANES), BF16), vmem((n_z, 2 * tiles, LANES), BF16),
             vmem((2, quarter, chans), BF16), vmem((2, quarter, chans), BF16),
             vmem((quarter, chans), BF16), vmem((quarter, chans), BF16),
             vmem((quarter, chans), BF16), vmem((n_taps, per, filt), F32),
             dma((4,)), dma((2,)), dma((2,)), dma((2,)),
-            dma((3, layer - 1)), dma((3, layer)), dma((2, n_z - 1)), dma((2, n_z)), dma((2,)), dma((2,)),
-            pltpu.SemaphoreType.REGULAR((3,)),
+            dma((5,)), dma((5,)), dma((2,)), dma((2,)), pltpu.SemaphoreType.REGULAR((3,)),
         ],
         compiler_params=pltpu.CompilerParams(
             collective_id=0, has_side_effects=True, vmem_limit_bytes=24 * 1024 * 1024

time: 39.4 us -> 38.4 us (0.975)
  the two profiles are of different devices: /device:TPU:16 before, /device:TPU:8 now
where the time goes in v3:
time: 38.4 us; the launch traced here: 38.3 us
  Pallas kernels  36.3 us (95%)
  local copies, waits for them, and re-layouts  1.27 us (3%)
  between operations  0.64 us (2%)
    pallas_call x1, Pallas kernels, on_device(): pl.pallas_call(functools.partial(kernel, sizes), out_shape=(jax.ShapeDtyp...  36.3 us
    unnamed x2, local copies, waits for them, and re-layouts  1.27 us

profile of v3, /device:TPU:8, one launch (start us, length us, event | category | flops | bytes accessed | tf_op | source)
XLA Modules:
  0.0 38.3 jit_solution(11132863403748114230)
XLA Ops:
  0.6 36.3 %conv_backward.1 = (bf16[256,256]{1,0:T(8,128)(2,1)S(1)}, f32[27,2,64]{2,1,0:T(2,128)S(1)}) custom-call(bf16[1024,256]{1,0:T(8,128)(2,1)} %bitcast.9, bf16[64,1024]{1,0:T(8,128)(2,1)} %bitcast.10, bf16[64,1024]{1,0:T(8,128)(2,1)} %bitcast.11, bf16[1728,256]{1,0:T(8,128)(2,1)} %bitcast.8), custom_call_target="tpu_custom_call" | custom-call | tf_op jit(solution)/shard_map/conv_backward/pallas_call | solution.py:274
  37.0 0.7 %copy.8 = bf16[1,8,32,256]{3,2,1,0:T(8,128)(2,1)} copy(bf16[1,8,32,256]{3,2,1,0:T(8,128)(2,1)S(1)} %bitcast.6) | data formatting | bytes 262144
  37.6 0.6 %copy.9 = f32[2,27,64]{2,0,1:T(2,128)} copy(f32[2,27,64]{2,0,1:T(2,128)S(1)} %bitcast.7) | data formatting | bytes 27648

commit v4 on v3

--- a/solution.py
+++ b/solution.py
@@ -52,7 +52,17 @@
 
     after = (space + 1) % n_space
     before = (space + n_space - 1) % n_space
-    layer_peers = [z_me * layer + (j_me + r) % layer for r in range(1, layer)]
+    row = layer // 2
+    y_low, x_me = j_me // row, j_me % row
+
+    def beside(dy, dx):
+        return ((y_low + dy) % 2) * row + (x_me + dx) % row
+
+    hops = sorted(
+        [(dy, dx) for dy in range(2) for dx in range(row) if dy or dx],
+        key=lambda d: -(d[0] + min(d[1], row - d[1])),
+    )
+    in_layer = [(beside(*d), z_me * layer + beside(*d)) for d in hops]
     far_first = sorted(range(1, n_z), key=lambda r: -min(r, n_z - r))
     core_peer = y_me * 2 + (1 - core)
     y_peer = (1 - y_me) * 2 + core
@@ -61,32 +71,39 @@
     def along_z(distance):
         return ((z_me + distance) % n_z) * layer + j_me
 
-    reach = 1
-    near_z = sorted({d for r in range(1, reach + 1) for d in (r, n_z - r)})
-    near = [after, before] + layer_peers + [along_z(d) for d in near_z]
+    crossing = {"space": z_me * layer + beside(1, 0), "filt": y_peer}
+    around = [{"space": z_me * layer + beside(*d)} for d in ((0, 1), (0, row - 1), (1, 0))] + [crossing]
+    near = around + [
+        {"space": peer} for peer in (after, before, along_z(1), along_z(n_z - 1))
+    ] + [{"filt": core_peer}]
     for peer in near:
-        pl.semaphore_signal(barrier, inc=1, device_id={"space": peer}, device_id_type=MESH)
-    for peer in (core_peer, y_peer):
-        pl.semaphore_signal(barrier, inc=1, device_id={"filt": peer}, device_id_type=MESH)
+        pl.semaphore_signal(barrier, inc=1, device_id=peer, device_id_type=MESH)
+
+    def round_of(i, peers):
+        def tell():
+            for peer in peers:
+                pl.semaphore_signal(known.at[i], inc=1, device_id=peer, device_id_type=MESH)
+
+        def learn():
+            if peers:
+                pl.semaphore_wait(known.at[i], len(peers))
+
+        return tell, learn
+
+    doubling = [1 << i for i in range(n_z.bit_length()) if (1 << i) < n_z // 2]
+    z_rounds = [
+        round_of(i, [{"space": along_z(d)} for d in (doubling[i], n_z - doubling[i])])
+        if i < len(doubling) else round_of(i, [])
+        for i in range(3)
+    ]
+    tell_around, learn_around = round_of(3, around)
+    tell_across, learn_across = round_of(4, around[2:3])
 
     def remote(src, dst, ssem, rsem, where):
         return pltpu.make_async_remote_copy(
             src_ref=src, dst_ref=dst, send_sem=ssem, recv_sem=rsem,
             device_id=where, device_id_type=MESH,
         )
-
-    reaches = [reach << i for i in range(n_z.bit_length()) if (reach << i) < n_z // 2]
-
-    def tell(i):
-        if i < len(reaches):
-            for distance in (reaches[i], n_z - reaches[i]):
-                pl.semaphore_signal(
-                    known.at[i], inc=1, device_id={"space": along_z(distance)}, device_id_type=MESH
-                )
-
-    def learn(i):
-        if i < len(reaches):
-            pl.semaphore_wait(known.at[i], 2)
 
     low = lax.broadcasted_iota(jnp.int32, (cells, LANES), 1) < filt
     col = lax.broadcasted_iota(jnp.int32, (cells, LANES), 0) % width
@@ -106,14 +123,15 @@
     d_pre = (og_ref[...].astype(F32) * silu_grad(pa_ref[...].astype(F32))).astype(BF16).astype(F32)
     twice = jnp.transpose(jnp.concatenate([d_pre, d_pre], axis=0))
     halo_out[...] = jnp.where(low[0:half], twice[0:half], twice[half:cells]).astype(BF16)
-    pl.semaphore_wait(barrier, len(near) + 2)
+    pl.semaphore_wait(barrier, len(near))
     halos = [
         remote(halo_out, halo_in.at[0], halo_ssem.at[0], halo_rsem.at[0], {"space": before}),
         remote(halo_out, halo_in.at[1], halo_ssem.at[1], halo_rsem.at[1], {"space": after}),
     ]
     for copy in halos:
         copy.start()
-    tell(0)
+    tell_around()
+    z_rounds[0][0]()
     fill(1, twice)
 
     loads[2].wait()
@@ -142,9 +160,10 @@
         g_out[a, :, per * full] = jnp.concatenate(
             [found[:, e, :, full * LANES :] for e in range(per)], axis=-1
         )
+
+    def share(a):
         exchange(a, g_out.at[a], g_in.at[a], j_me, in_layer)
 
-    in_layer = [((j_me + r) % layer, peer) for r, peer in zip(range(1, layer), layer_peers)]
     in_column = [((z_me + d) % n_z, along_z(d)) for d in far_first]
 
     def exchange(part, out, into, me, peers):
@@ -158,9 +177,13 @@
         others = into.at[pl.ds(0, into.shape[0] - 1)]
         pltpu.make_async_copy(others, others, sem).wait()
 
+    learn_around()
+    tell_across()
     taps(1)
-    learn(0)
-    tell(1)
+    learn_across()
+    share(1)
+    z_rounds[0][1]()
+    z_rounds[1][0]()
 
     def products(q, a):
         total = None
@@ -189,8 +212,9 @@
             [jnp.where(low[0:half], packed, turned), jnp.where(low[0:half], turned, packed)], axis=0
         ))
         taps(2 * i)
-    learn(1)
-    tell(2)
+        share(2 * i)
+    z_rounds[1][1]()
+    z_rounds[2][0]()
 
     for q in range(4):
         gi_acc[q] = gi_acc[q] + products(q, 0) + products(q, 2)
@@ -224,7 +248,7 @@
 
     gather(1, 0)
     m_out[...] = z_wide[:, 0:tiles, :].astype(BF16)
-    learn(2)
+    z_rounds[2][1]()
     exchange(3, m_out, m_in, z_me, in_column)
 
     cores.wait_recv()
@@ -257,6 +281,17 @@
         copy.wait_send()
     store_gi.wait()
     store_gw.wait()
+
+
+def hand_over(gi_ref, gw_ref, gi_out, gw_out, sem):
+    copies = [
+        pltpu.make_async_copy(gi_ref, gi_out, sem.at[0]),
+        pltpu.make_async_copy(gw_ref, gw_out, sem.at[1]),
+    ]
+    for copy in copies:
+        copy.start()
+    for copy in copies:
+        copy.wait()
 
 
 def on_device(layer, inputs, out_grad, pre_act, weight):
@@ -271,14 +306,16 @@
     sizes = (n_space, layer, height, width, chans, filt)
     dma = pltpu.SemaphoreType.DMA
     vmem = pltpu.VMEM
-    grad_input, grad_weight = pl.pallas_call(
+    shapes = (
+        jax.ShapeDtypeStruct((quarter, chans), BF16),
+        jax.ShapeDtypeStruct((n_taps, per, filt), F32),
+    )
+    anywhere = pl.BlockSpec(memory_space=pl.ANY)
+    found = pl.pallas_call(
         functools.partial(kernel, sizes),
-        out_shape=(
-            jax.ShapeDtypeStruct((quarter, chans), BF16),
-            jax.ShapeDtypeStruct((n_taps, per, filt), F32),
-        ),
+        out_shape=shapes,
         in_specs=[pl.BlockSpec(memory_space=pltpu.HBM)] * 4,
-        out_specs=(pl.BlockSpec(memory_space=pl.ANY),) * 2,
+        out_specs=(anywhere,) * 2,
         scratch_shapes=[
             vmem((cells, chans), BF16), vmem((filt, cells), BF16), vmem((filt, cells), BF16),
             vmem((n_taps * filt, chans), BF16), vmem((chans, cells), BF16),
@@ -292,7 +329,7 @@
             vmem((quarter, chans), BF16), vmem((quarter, chans), BF16),
             vmem((quarter, chans), BF16), vmem((n_taps, per, filt), F32),
             dma((4,)), dma((2,)), dma((2,)), dma((2,)),
-            dma((5,)), dma((5,)), dma((2,)), dma((2,)), pltpu.SemaphoreType.REGULAR((3,)),
+            dma((5,)), dma((5,)), dma((2,)), dma((2,)), pltpu.SemaphoreType.REGULAR((5,)),
         ],
         compiler_params=pltpu.CompilerParams(
             collective_id=0, has_side_effects=True, vmem_limit_bytes=24 * 1024 * 1024
@@ -307,6 +344,15 @@
             )
         ]
     )
+    grad_input, grad_weight = pl.pallas_call(
+        hand_over,
+        out_shape=shapes,
+        in_specs=[anywhere] * 2,
+        out_specs=(anywhere,) * 2,
+        scratch_shapes=[dma((2,))],
+        compiler_params=pltpu.CompilerParams(vmem_limit_bytes=1024 * 1024),
+        name="hand_over",
+    )(*found)
     return grad_input.reshape(1, height // 4, width, chans), jnp.swapaxes(grad_weight, 0, 1)
 
 

time: 38.4 us -> 37.9 us (0.987)
  the two profiles are of different devices: /device:TPU:8 before, /device:TPU:16 now
where the time goes in v4:
time: 37.9 us; the launch traced here: 37.7 us
  Pallas kernels  37.1 us (98%)
  between operations  0.64 us (2%)
    pallas_call x1, Pallas kernels, on_device(): pl.pallas_call(functools.partial(kernel, sizes), out_shape=shapes, in_spe...  36.4 us

profile of v4, /device:TPU:16, one launch (start us, length us, event | category | flops | bytes accessed | tf_op | source)
XLA Modules:
  0.0 37.7 jit_solution(8972188398844557695)
XLA Ops:
  0.6 36.4 %conv_backward.1 = (bf16[256,256]{1,0:T(8,128)(2,1)S(1)}, f32[27,2,64]{2,1,0:T(2,128)S(1)}) custom-call(bf16[1024,256]{1,0:T(8,128)(2,1)} %bitcast.7, bf16[64,1024]{1,0:T(8,128)(2,1)} %bitcast.8, bf16[64,1024]{1,0:T(8,128)(2,1)} %bitcast.9, bf16[1728,256]{1,0:T(8,128)(2,1)} %bitcast.6), custom_call_target="tpu_custom_call" | custom-call | tf_op jit(solution)/shard_map/conv_backward/pallas_call | solution.py:314
  37.1 0.7 %hand_over.1 = (bf16[256,256]{1,0:T(8,128)(2,1)}, f32[27,2,64]{2,1,0:T(2,128)}) custom-call(bf16[256,256]{1,0:T(8,128)(2,1)S(1)} %get-tuple-element.6.gi_ref, f32[27,2,64]{2,1,0:T(2,128)S(1)} %get-tuple-element.7.gw_ref), custom_call_target="tpu_custom_call" | custom-call | tf_op jit(solution)/shard_map/hand_over/pallas_call | solution.py:347

commit v5 on v4

--- a/solution.py
+++ b/solution.py
@@ -22,7 +22,7 @@
 def kernel(
     sizes, x_hbm, og_hbm, pa_hbm, w_hbm, gi_hbm, gw_hbm,
     x_ref, og_ref, pa_ref, w_ref, xt_ref, buf, gi_acc,
-    halo_out, halo_in, g_out, g_in, z_wide, m_out, m_in, e_out, e_in,
+    halo_out, halo_in, b_out, b_in, a_out, a_in, b_wide, a_wide, m_out, m_in, e_out, e_in,
     c_out, c_in, y_out, y_in, gi_ref, gw_ref,
     load_sem, store_sem, halo_ssem, halo_rsem, many_ssem, many_rsem, f_ssem, f_rsem, known,
 ):
@@ -32,8 +32,10 @@
     quarter = cells // 4
     per = chans // n_space
     rows_j = per * n_z
-    tiles = g_out.shape[2]
+    tiles = b_out.shape[1]
     full = tiles // per
+    near_rows = n_z // 2
+    turn_z = n_z // 4
     lanes3 = 3 * filt
 
     space = lax.axis_index("space")
@@ -63,7 +65,7 @@
         key=lambda d: -(d[0] + min(d[1], row - d[1])),
     )
     in_layer = [(beside(*d), z_me * layer + beside(*d)) for d in hops]
-    far_first = sorted(range(1, n_z), key=lambda r: -min(r, n_z - r))
+    steps = [(turn_z + i) % n_z for i in range(n_z)]
     core_peer = y_me * 2 + (1 - core)
     y_peer = (1 - y_me) * 2 + core
 
@@ -137,51 +139,64 @@
     loads[2].wait()
     r = lax.broadcasted_iota(jnp.int32, (chans, chans), 0)
     k = lax.broadcasted_iota(jnp.int32, (chans, chans), 1)
-    source = per * layer * (r % n_z) + per * (r // rows_j) + (r // n_z) % per
+    source = per * layer * ((z_me + turn_z + r % n_z) % n_z) + per * (r // rows_j) + (r // n_z) % per
     pick = jnp.where(k == source, 1.0, 0.0).astype(BF16)
     xt_ref[...] = lax.dot_general(
         pick, x_ref[...], (((1,), (1,)), ((), ())), preferred_element_type=F32
     ).astype(BF16)
 
     def taps(a):
-        found = jnp.concatenate(
+        return jnp.concatenate(
             [
                 jnp.dot(
                     xt_ref[...], buf[a, (2 - b) * width : (2 - b) * width + cells, :],
                     preferred_element_type=F32,
-                ).astype(BF16)
+                )
                 for b in range(3)
             ],
             axis=1,
-        ).reshape(layer, per, n_z, 9 * filt)
+        )
+
+    def pieces(rows_of, write):
         for e in range(per):
             for l in range(full):
-                g_out[a, :, e * full + l] = found[:, e, :, l * LANES : (l + 1) * LANES]
-        g_out[a, :, per * full] = jnp.concatenate(
-            [found[:, e, :, full * LANES :] for e in range(per)], axis=-1
-        )
-
-    def share(a):
-        exchange(a, g_out.at[a], g_in.at[a], j_me, in_layer)
-
-    in_column = [((z_me + d) % n_z, along_z(d)) for d in far_first]
-
-    def exchange(part, out, into, me, peers):
-        for slot, peer in peers:
+                write(e * full + l, rows_of(e)[:, :, l * LANES : (l + 1) * LANES])
+        write(per * full, jnp.concatenate(
+            [rows_of(e)[:, :, full * LANES :] for e in range(per)], axis=-1
+        ))
+
+    def exchange(part, out, into, peers):
+        for slot, landing, peer in peers:
             remote(
-                out.at[slot], into.at[me], many_ssem.at[part], many_rsem.at[part], {"space": peer}
+                out.at[slot], into.at[landing], many_ssem.at[part], many_rsem.at[part], {"space": peer}
             ).start()
-        into[me] = out[me]
-
-    def all_of(into, sem):
-        others = into.at[pl.ds(0, into.shape[0] - 1)]
+
+    def share(part, out, into):
+        exchange(part, out, into, [(slot, j_me, peer) for slot, peer in in_layer])
+        into[j_me] = out[j_me]
+
+    def send_along(part, out, into, rows):
+        found = [i for i in rows if steps[i]]
+        found.sort(key=lambda i: -min(steps[i], n_z - steps[i]))
+        exchange(part, out, into, [(i - rows[0], i - rows[0], along_z(steps[i])) for i in found])
+        for i in rows:
+            if not steps[i]:
+                into[i - rows[0]] = out[i - rows[0]]
+
+    def all_of(into, sem, count):
+        others = into.at[pl.ds(0, count)]
         pltpu.make_async_copy(others, others, sem).wait()
 
     learn_around()
     tell_across()
-    taps(1)
+    found = taps(1).astype(BF16).reshape(layer, per, n_z, 9 * filt)
+
+    def write_b(tile, value):
+        b_out[:, tile] = value
+
+    pieces(lambda e: found[:, e], write_b)
     learn_across()
-    share(1)
+    share(0, b_out, b_in)
     z_rounds[0][1]()
     z_rounds[1][0]()
 
@@ -211,8 +226,15 @@
         fill(2 * i, jnp.concatenate(
             [jnp.where(low[0:half], packed, turned), jnp.where(low[0:half], turned, packed)], axis=0
         ))
-        taps(2 * i)
-        share(2 * i)
+        found = taps(2 * i).reshape(layer, per, 2, near_rows, 9 * filt)
+        for side in range(2):
+
+            def write_a(tile, value):
+                a_out[side, :, i * tiles + tile] = value.astype(BF16)
+
+            pieces(lambda e: found[:, e, side], write_a)
+    for side in range(2):
+        share(1 + side, a_out.at[side], a_in.at[side])
     z_rounds[1][1]()
     z_rounds[2][0]()
 
@@ -223,19 +245,21 @@
     cores = remote(c_out, c_in, f_ssem.at[0], f_rsem.at[0], {"filt": core_peer})
     cores.start()
 
-    def gather(a, base):
-        all_of(g_in.at[a], many_rsem.at[a])
-        for t in range(tiles):
-            total = g_in[a, 0, t].astype(F32)
+    def gather(part, into, wide):
+        all_of(into, many_rsem.at[part], layer - 1)
+        for t in range(into.shape[1]):
+            total = into[0, t].astype(F32)
             for j in range(1, layer):
-                total = total + g_in[a, j, t].astype(F32)
-            z_wide[:, base + t, :] = total
+                total = total + into[j, t].astype(F32)
+            wide[:, t, :] = total
 
     def summed(into):
         total = into[0].astype(F32)
         for z in range(1, into.shape[0]):
             total = total + into[z].astype(F32)
-        return total * (float(cells * n_space) ** -0.5)
+        return total
+
+    scale = float(cells * n_space) ** -0.5
 
     def place(total, base, a):
         for e in range(per):
@@ -244,39 +268,45 @@
                     row, part = base + e * full + tap // 2, tap % 2
                 else:
                     row, part = base + per * full, e
-                gw_ref[9 * a + tap, e : e + 1, :] = total[row : row + 1, part * filt : (part + 1) * filt]
-
-    gather(1, 0)
-    m_out[...] = z_wide[:, 0:tiles, :].astype(BF16)
+                gw_ref[9 * a + tap, e : e + 1, :] = scale * total[row : row + 1, part * filt : (part + 1) * filt]
+
+    gather(0, b_in, b_wide)
+    m_out[...] = b_wide[...].astype(BF16)
     z_rounds[2][1]()
-    exchange(3, m_out, m_in, z_me, in_column)
+    send_along(3, m_out, m_in, range(n_z))
 
     cores.wait_recv()
     y_out[...] = (gi_acc[2 * (1 - y_me) + core] + c_in[1 - y_me].astype(F32)).astype(BF16)
     ys = remote(y_out, y_in, f_ssem.at[1], f_rsem.at[1], {"filt": y_peer})
     ys.start()
 
-    gather(0, 0)
-    gather(2, tiles)
-    e_out[...] = z_wide[...].astype(BF16)
-    exchange(4, e_out, e_in, z_me, in_column)
+    for side in range(2):
+        gather(1 + side, a_in.at[side], a_wide)
+        e_out[side] = a_wide[...].astype(BF16)
+        rows = range(side * near_rows, (side + 1) * near_rows)
+        send_along(4 + side, e_out.at[side], e_in.at[side], rows)
 
     ys.wait_recv()
     gi_ref[...] = (gi_acc[2 * y_me + core] + c_in[y_me].astype(F32) + y_in[...].astype(F32)).astype(BF16)
     store_gi = pltpu.make_async_copy(gi_ref, gi_hbm, store_sem.at[0])
     store_gi.start()
 
-    all_of(m_in, many_rsem.at[3])
+    all_of(m_in, many_rsem.at[3], n_z - 1)
     place(summed(m_in), 0, 1)
-    all_of(e_in, many_rsem.at[4])
-    total = summed(e_in)
+    all_of(e_in.at[0], many_rsem.at[4], near_rows)
+    total = summed(e_in.at[0])
+    all_of(e_in.at[1], many_rsem.at[5], near_rows - 1)
+    total = total + summed(e_in.at[1])
     place(total, 0, 0)
     place(total, tiles, 2)
     store_gw = pltpu.make_async_copy(gw_ref, gw_hbm, store_sem.at[1])
     store_gw.start()
 
-    for part, out in enumerate((g_out.at[0], g_out.at[1], g_out.at[2], m_out, e_out)):
-        all_of(out, many_ssem.at[part])
+    for part, out in enumerate((b_out, a_out.at[0], a_out.at[1])):
+        all_of(out, many_ssem.at[part], layer - 1)
+    all_of(m_out, many_ssem.at[3], n_z - 1)
+    all_of(e_out.at[0], many_ssem.at[4], near_rows)
+    all_of(e_out.at[1], many_ssem.at[5], near_rows - 1)
     for copy in halos + [cores, ys]:
         copy.wait_send()
     store_gi.wait()
@@ -321,15 +351,16 @@
             vmem((n_taps * filt, chans), BF16), vmem((chans, cells), BF16),
             vmem((3, cells + 2 * width, 3 * filt), BF16), vmem((4, quarter, chans), F32),
             vmem((cells // 2, LANES), BF16), vmem((2, cells // 2, LANES), BF16),
-            vmem((3, layer, tiles, n_z, LANES), BF16), vmem((3, layer, tiles, n_z, LANES), BF16),
-            vmem((n_z, 2 * tiles, LANES), F32),
+            vmem((layer, tiles, n_z, LANES), BF16), vmem((layer, tiles, n_z, LANES), BF16),
+            vmem((2, layer, 2 * tiles, n_z // 2, LANES), BF16), vmem((2, layer, 2 * tiles, n_z // 2, LANES), BF16),
+            vmem((n_z, tiles, LANES), F32), vmem((n_z // 2, 2 * tiles, LANES), F32),
             vmem((n_z, tiles, LANES), BF16), vmem((n_z, tiles, LANES), BF16),
-            vmem((n_z, 2 * tiles, LANES), BF16), vmem((n_z, 2 * tiles, LANES), BF16),
+            vmem((2, n_z // 2, 2 * tiles, LANES), BF16), vmem((2, n_z // 2, 2 * tiles, LANES), BF16),
             vmem((2, quarter, chans), BF16), vmem((2, quarter, chans), BF16),
             vmem((quarter, chans), BF16), vmem((quarter, chans), BF16),
             vmem((quarter, chans), BF16), vmem((n_taps, per, filt), F32),
             dma((4,)), dma((2,)), dma((2,)), dma((2,)),
-            dma((5,)), dma((5,)), dma((2,)), dma((2,)), pltpu.SemaphoreType.REGULAR((5,)),
+            dma((6,)), dma((6,)), dma((2,)), dma((2,)), pltpu.SemaphoreType.REGULAR((5,)),
         ],
         compiler_params=pltpu.CompilerParams(
             collective_id=0, has_side_effects=True, vmem_limit_bytes=24 * 1024 * 1024

time: 37.9 us -> 37.1 us (0.979)
  the two profiles are of different devices: /device:TPU:16 before, /device:TPU:30 now
where the time goes in v5:
time: 37.1 us; the launch traced here: 36.9 us
  Pallas kernels  36.3 us (98%)
  between operations  0.64 us (2%)
    pallas_call x1, Pallas kernels, on_device(): pl.pallas_call(functools.partial(kernel, sizes), out_shape=shapes, in_spe...  35.6 us

profile of v5, /device:TPU:30, one launch (start us, length us, event | category | flops | bytes accessed | tf_op | source)
XLA Modules:
  0.0 36.9 jit_solution(1723554687961468012)
XLA Ops:
  0.6 35.6 %conv_backward.1 = (bf16[256,256]{1,0:T(8,128)(2,1)S(1)}, f32[27,2,64]{2,1,0:T(2,128)S(1)}) custom-call(bf16[1024,256]{1,0:T(8,128)(2,1)} %bitcast.7, bf16[64,1024]{1,0:T(8,128)(2,1)} %bitcast.8, bf16[64,1024]{1,0:T(8,128)(2,1)} %bitcast.9, bf16[1728,256]{1,0:T(8,128)(2,1)} %bitcast.6), custom_call_target="tpu_custom_call" | custom-call | tf_op jit(solution)/shard_map/conv_backward/pallas_call | solution.py:344
  36.2 0.7 %hand_over.1 = (bf16[256,256]{1,0:T(8,128)(2,1)}, f32[27,2,64]{2,1,0:T(2,128)}) custom-call(bf16[256,256]{1,0:T(8,128)(2,1)S(1)} %get-tuple-element.6.gi_ref, f32[27,2,64]{2,1,0:T(2,128)S(1)} %get-tuple-element.7.gw_ref), custom_call_target="tpu_custom_call" | custom-call | tf_op jit(solution)/shard_map/hand_over/pallas_call | solution.py:378

commit v6 on v5

--- a/solution.py
+++ b/solution.py
@@ -73,11 +73,10 @@
     def along_z(distance):
         return ((z_me + distance) % n_z) * layer + j_me
 
-    crossing = {"space": z_me * layer + beside(1, 0), "filt": y_peer}
-    around = [{"space": z_me * layer + beside(*d)} for d in ((0, 1), (0, row - 1), (1, 0))] + [crossing]
-    near = around + [
-        {"space": peer} for peer in (after, before, along_z(1), along_z(n_z - 1))
-    ] + [{"filt": core_peer}]
+    near = [
+        {"space": peer}
+        for peer in [after, before, along_z(1), along_z(n_z - 1)] + [peer for _, peer in in_layer]
+    ] + [{"filt": core_peer}, {"filt": y_peer}]
     for peer in near:
         pl.semaphore_signal(barrier, inc=1, device_id=peer, device_id_type=MESH)
 
@@ -98,8 +97,6 @@
         if i < len(doubling) else round_of(i, [])
         for i in range(3)
     ]
-    tell_around, learn_around = round_of(3, around)
-    tell_across, learn_across = round_of(4, around[2:3])
 
     def remote(src, dst, ssem, rsem, where):
         return pltpu.make_async_remote_copy(
@@ -132,7 +129,6 @@
     ]
     for copy in halos:
         copy.start()
-    tell_around()
     z_rounds[0][0]()
     fill(1, twice)
 
@@ -187,15 +183,12 @@
         others = into.at[pl.ds(0, count)]
         pltpu.make_async_copy(others, others, sem).wait()
 
-    learn_around()
-    tell_across()
     found = taps(1).astype(BF16).reshape(layer, per, n_z, 9 * filt)
 
     def write_b(tile, value):
         b_out[:, tile] = value
 
     pieces(lambda e: found[:, e], write_b)
-    learn_across()
     share(0, b_out, b_in)
     z_rounds[0][1]()
     z_rounds[1][0]()
@@ -230,11 +223,12 @@
         for side in range(2):
 
             def write_a(tile, value):
-                a_out[side, :, i * tiles + tile] = value.astype(BF16)
+                a_out[side, i, :, tile] = value.astype(BF16)
 
             pieces(lambda e: found[:, e, side], write_a)
-    for side in range(2):
-        share(1 + side, a_out.at[side], a_in.at[side])
+        share(6 + i, a_out.at[0, i], a_in.at[0, i])
+    for i in range(2):
+        share(1 + i, a_out.at[1, i], a_in.at[1, i])
     z_rounds[1][1]()
     z_rounds[2][0]()
 
@@ -245,13 +239,13 @@
     cores = remote(c_out, c_in, f_ssem.at[0], f_rsem.at[0], {"filt": core_peer})
     cores.start()
 
-    def gather(part, into, wide):
+    def gather(part, into, wide, base=0):
         all_of(into, many_rsem.at[part], layer - 1)
         for t in range(into.shape[1]):
             total = into[0, t].astype(F32)
             for j in range(1, layer):
                 total = total + into[j, t].astype(F32)
-            wide[:, t, :] = total
+            wide[:, base + t, :] = total
 
     def summed(into):
         total = into[0].astype(F32)
@@ -281,7 +275,8 @@
     ys.start()
 
     for side in range(2):
-        gather(1 + side, a_in.at[side], a_wide)
+        for i in range(2):
+            gather((6, 1)[side] + i, a_in.at[side, i], a_wide, i * tiles)
         e_out[side] = a_wide[...].astype(BF16)
         rows = range(side * near_rows, (side + 1) * near_rows)
         send_along(4 + side, e_out.at[side], e_in.at[side], rows)
@@ -302,8 +297,10 @@
     store_gw = pltpu.make_async_copy(gw_ref, gw_hbm, store_sem.at[1])
     store_gw.start()
 
-    for part, out in enumerate((b_out, a_out.at[0], a_out.at[1])):
-        all_of(out, many_ssem.at[part], layer - 1)
+    all_of(b_out, many_ssem.at[0], layer - 1)
+    for i in range(2):
+        all_of(a_out.at[0, i], many_ssem.at[6 + i], layer - 1)
+        all_of(a_out.at[1, i], many_ssem.at[1 + i], layer - 1)
     all_of(m_out, many_ssem.at[3], n_z - 1)
     all_of(e_out.at[0], many_ssem.at[4], near_rows)
     all_of(e_out.at[1], many_ssem.at[5], near_rows - 1)
@@ -352,7 +349,7 @@
             vmem((3, cells + 2 * width, 3 * filt), BF16), vmem((4, quarter, chans), F32),
             vmem((cells // 2, LANES), BF16), vmem((2, cells // 2, LANES), BF16),
             vmem((layer, tiles, n_z, LANES), BF16), vmem((layer, tiles, n_z, LANES), BF16),
-            vmem((2, layer, 2 * tiles, n_z // 2, LANES), BF16), vmem((2, layer, 2 * tiles, n_z // 2, LANES), BF16),
+            vmem((2, 2, layer, tiles, n_z // 2, LANES), BF16), vmem((2, 2, layer, tiles, n_z // 2, LANES), BF16),
             vmem((n_z, tiles, LANES), F32), vmem((n_z // 2, 2 * tiles, LANES), F32),
             vmem((n_z, tiles, LANES), BF16), vmem((n_z, tiles, LANES), BF16),
             vmem((2, n_z // 2, 2 * tiles, LANES), BF16), vmem((2, n_z // 2, 2 * tiles, LANES), BF16),
@@ -360,7 +357,7 @@
             vmem((quarter, chans), BF16), vmem((quarter, chans), BF16),
             vmem((quarter, chans), BF16), vmem((n_taps, per, filt), F32),
             dma((4,)), dma((2,)), dma((2,)), dma((2,)),
-            dma((6,)), dma((6,)), dma((2,)), dma((2,)), pltpu.SemaphoreType.REGULAR((5,)),
+            dma((8,)), dma((8,)), dma((2,)), dma((2,)), pltpu.SemaphoreType.REGULAR((3,)),
         ],
         compiler_params=pltpu.CompilerParams(
             collective_id=0, has_side_effects=True, vmem_limit_bytes=24 * 1024 * 1024

time: 37.1 us -> 36.1 us (0.973)
  the two profiles are of different devices: /device:TPU:30 before, /device:TPU:8 now
where the time goes in v6:
time: 36.1 us; the launch traced here: 36 us
  Pallas kernels  35.3 us (98%)
  between operations  0.64 us (2%)
    pallas_call x1, Pallas kernels, on_device(): pl.pallas_call(functools.partial(kernel, sizes), out_shape=shapes, in_spe...  34.6 us

profile of v6, /device:TPU:8, one launch (start us, length us, event | category | flops | bytes accessed | tf_op | source)
XLA Modules:
  0.0 36.0 jit_solution(10556623962243193885)
XLA Ops:
  0.6 34.6 %conv_backward.1 = (bf16[256,256]{1,0:T(8,128)(2,1)S(1)}, f32[27,2,64]{2,1,0:T(2,128)S(1)}) custom-call(bf16[1024,256]{1,0:T(8,128)(2,1)} %bitcast.7, bf16[64,1024]{1,0:T(8,128)(2,1)} %bitcast.8, bf16[64,1024]{1,0:T(8,128)(2,1)} %bitcast.9, bf16[1728,256]{1,0:T(8,128)(2,1)} %bitcast.6), custom_call_target="tpu_custom_call" | custom-call | tf_op jit(solution)/shard_map/conv_backward/pallas_call | solution.py:341
  35.3 0.7 %hand_over.1 = (bf16[256,256]{1,0:T(8,128)(2,1)}, f32[27,2,64]{2,1,0:T(2,128)}) custom-call(bf16[256,256]{1,0:T(8,128)(2,1)S(1)} %get-tuple-element.6.gi_ref, f32[27,2,64]{2,1,0:T(2,128)S(1)} %get-tuple-element.7.gw_ref), custom_call_target="tpu_custom_call" | custom-call | tf_op jit(solution)/shard_map/hand_over/pallas_call | solution.py:375

commit v7 on v6

--- a/solution.py
+++ b/solution.py
@@ -22,7 +22,7 @@
 def kernel(
     sizes, x_hbm, og_hbm, pa_hbm, w_hbm, gi_hbm, gw_hbm,
     x_ref, og_ref, pa_ref, w_ref, xt_ref, buf, gi_acc,
-    halo_out, halo_in, b_out, b_in, a_out, a_in, b_wide, a_wide, m_out, m_in, e_out, e_in,
+    halo_out, halo_in, a_out, a_in, a_wide, e_out, e_in,
     c_out, c_in, y_out, y_in, gi_ref, gw_ref,
     load_sem, store_sem, halo_ssem, halo_rsem, many_ssem, many_rsem, f_ssem, f_rsem, known,
 ):
@@ -32,7 +32,7 @@
     quarter = cells // 4
     per = chans // n_space
     rows_j = per * n_z
-    tiles = b_out.shape[1]
+    tiles = a_out.shape[3]
     full = tiles // per
     near_rows = n_z // 2
     turn_z = n_z // 4
@@ -183,13 +183,20 @@
         others = into.at[pl.ds(0, count)]
         pltpu.make_async_copy(others, others, sem).wait()
 
-    found = taps(1).astype(BF16).reshape(layer, per, n_z, 9 * filt)
-
-    def write_b(tile, value):
-        b_out[:, tile] = value
-
-    pieces(lambda e: found[:, e], write_b)
-    share(0, b_out, b_in)
+    def prepare(a):
+        found = taps(a).reshape(layer, per, 2, near_rows, 9 * filt)
+        for side in range(2):
+
+            def write(tile, value):
+                a_out[side, a, :, tile] = value.astype(BF16)
+
+            pieces(lambda e: found[:, e, side], write)
+
+    def share_side(side, a):
+        share(3 * side + a, a_out.at[side, a], a_in.at[side, a])
+
+    prepare(1)
+    share_side(0, 1)
     z_rounds[0][1]()
     z_rounds[1][0]()
 
@@ -219,16 +226,8 @@
         fill(2 * i, jnp.concatenate(
             [jnp.where(low[0:half], packed, turned), jnp.where(low[0:half], turned, packed)], axis=0
         ))
-        found = taps(2 * i).reshape(layer, per, 2, near_rows, 9 * filt)
-        for side in range(2):
-
-            def write_a(tile, value):
-                a_out[side, i, :, tile] = value.astype(BF16)
-
-            pieces(lambda e: found[:, e, side], write_a)
-        share(6 + i, a_out.at[0, i], a_in.at[0, i])
-    for i in range(2):
-        share(1 + i, a_out.at[1, i], a_in.at[1, i])
+        prepare(2 * i)
+        share_side(0, 2 * i)
     z_rounds[1][1]()
     z_rounds[2][0]()
 
@@ -238,6 +237,8 @@
         c_out[y] = gi_acc[2 * y + (1 - core)].astype(BF16)
     cores = remote(c_out, c_in, f_ssem.at[0], f_rsem.at[0], {"filt": core_peer})
     cores.start()
+    for a in (1, 0, 2):
+        share_side(1, a)
 
     def gather(part, into, wide, base=0):
         all_of(into, many_rsem.at[part], layer - 1)
@@ -264,46 +265,38 @@
                     row, part = base + per * full, e
                 gw_ref[9 * a + tap, e : e + 1, :] = scale * total[row : row + 1, part * filt : (part + 1) * filt]
 
-    gather(0, b_in, b_wide)
-    m_out[...] = b_wide[...].astype(BF16)
-    z_rounds[2][1]()
-    send_along(3, m_out, m_in, range(n_z))
-
     cores.wait_recv()
     y_out[...] = (gi_acc[2 * (1 - y_me) + core] + c_in[1 - y_me].astype(F32)).astype(BF16)
     ys = remote(y_out, y_in, f_ssem.at[1], f_rsem.at[1], {"filt": y_peer})
     ys.start()
 
     for side in range(2):
-        for i in range(2):
-            gather((6, 1)[side] + i, a_in.at[side, i], a_wide, i * tiles)
+        for a in (1, 0, 2):
+            gather(3 * side + a, a_in.at[side, a], a_wide, a * tiles)
         e_out[side] = a_wide[...].astype(BF16)
         rows = range(side * near_rows, (side + 1) * near_rows)
-        send_along(4 + side, e_out.at[side], e_in.at[side], rows)
+        if side == 0:
+            z_rounds[2][1]()
+        send_along(6 + side, e_out.at[side], e_in.at[side], rows)
 
     ys.wait_recv()
     gi_ref[...] = (gi_acc[2 * y_me + core] + c_in[y_me].astype(F32) + y_in[...].astype(F32)).astype(BF16)
     store_gi = pltpu.make_async_copy(gi_ref, gi_hbm, store_sem.at[0])
     store_gi.start()
 
-    all_of(m_in, many_rsem.at[3], n_z - 1)
-    place(summed(m_in), 0, 1)
-    all_of(e_in.at[0], many_rsem.at[4], near_rows)
+    all_of(e_in.at[0], many_rsem.at[6], near_rows)
     total = summed(e_in.at[0])
-    all_of(e_in.at[1], many_rsem.at[5], near_rows - 1)
+    all_of(e_in.at[1], many_rsem.at[7], near_rows - 1)
     total = total + summed(e_in.at[1])
-    place(total, 0, 0)
-    place(total, tiles, 2)
+    for a in range(3):
+        place(total, a * tiles, a)
     store_gw = pltpu.make_async_copy(gw_ref, gw_hbm, store_sem.at[1])
     store_gw.start()
 
-    all_of(b_out, many_ssem.at[0], layer - 1)
-    for i in range(2):
-        all_of(a_out.at[0, i], many_ssem.at[6 + i], layer - 1)
-        all_of(a_out.at[1, i], many_ssem.at[1 + i], layer - 1)
-    all_of(m_out, many_ssem.at[3], n_z - 1)
-    all_of(e_out.at[0], many_ssem.at[4], near_rows)
-    all_of(e_out.at[1], many_ssem.at[5], near_rows - 1)
+    for side in range(2):
+        for a in range(3):
+            all_of(a_out.at[side, a], many_ssem.at[3 * side + a], layer - 1)
+        all_of(e_out.at[side], many_ssem.at[6 + side], near_rows - side)
     for copy in halos + [cores, ys]:
         copy.wait_send()
     store_gi.wait()
@@ -348,11 +341,9 @@
             vmem((n_taps * filt, chans), BF16), vmem((chans, cells), BF16),
             vmem((3, cells + 2 * width, 3 * filt), BF16), vmem((4, quarter, chans), F32),
             vmem((cells // 2, LANES), BF16), vmem((2, cells // 2, LANES), BF16),
-            vmem((layer, tiles, n_z, LANES), BF16), vmem((layer, tiles, n_z, LANES), BF16),
-            vmem((2, 2, layer, tiles, n_z // 2, LANES), BF16), vmem((2, 2, layer, tiles, n_z // 2, LANES), BF16),
-            vmem((n_z, tiles, LANES), F32), vmem((n_z // 2, 2 * tiles, LANES), F32),
-            vmem((n_z, tiles, LANES), BF16), vmem((n_z, tiles, LANES), BF16),
-            vmem((2, n_z // 2, 2 * tiles, LANES), BF16), vmem((2, n_z // 2, 2 * tiles, LANES), BF16),
+            vmem((2, 3, layer, tiles, n_z // 2, LANES), BF16), vmem((2, 3, layer, tiles, n_z // 2, LANES), BF16),
+            vmem((n_z // 2, 3 * tiles, LANES), F32),
+            vmem((2, n_z // 2, 3 * tiles, LANES), BF16), vmem((2, n_z // 2, 3 * tiles, LANES), BF16),
             vmem((2, quarter, chans), BF16), vmem((2, quarter, chans), BF16),
             vmem((quarter, chans), BF16), vmem((quarter, chans), BF16),
             vmem((quarter, chans), BF16), vmem((n_taps, per, filt), F32),

time: 36.1 us -> 35.6 us (0.986)
  the two profiles are of different devices: /device:TPU:8 before, /device:TPU:32 now
where the time goes in v7:
time: 35.6 us; the launch traced here: 35.5 us
  Pallas kernels  34.8 us (98%)
  between operations  0.64 us (2%)
    pallas_call x1, Pallas kernels, on_device(): pl.pallas_call(functools.partial(kernel, sizes), out_shape=shapes, in_spe...  34.1 us

profile of v7, /device:TPU:32, one launch (start us, length us, event | category | flops | bytes accessed | tf_op | source)
XLA Modules:
  0.0 35.5 jit_solution(13029508771348900809)
XLA Ops:
  0.6 34.1 %conv_backward.1 = (bf16[256,256]{1,0:T(8,128)(2,1)S(1)}, f32[27,2,64]{2,1,0:T(2,128)S(1)}) custom-call(bf16[1024,256]{1,0:T(8,128)(2,1)} %bitcast.7, bf16[64,1024]{1,0:T(8,128)(2,1)} %bitcast.8, bf16[64,1024]{1,0:T(8,128)(2,1)} %bitcast.9, bf16[1728,256]{1,0:T(8,128)(2,1)} %bitcast.6), custom_call_target="tpu_custom_call" | custom-call | tf_op jit(solution)/shard_map/conv_backward/pallas_call | solution.py:334
  34.8 0.7 %hand_over.1 = (bf16[256,256]{1,0:T(8,128)(2,1)}, f32[27,2,64]{2,1,0:T(2,128)}) custom-call(bf16[256,256]{1,0:T(8,128)(2,1)S(1)} %get-tuple-element.6.gi_ref, f32[27,2,64]{2,1,0:T(2,128)S(1)} %get-tuple-element.7.gw_ref), custom_call_target="tpu_custom_call" | custom-call | tf_op jit(solution)/shard_map/hand_over/pallas_call | solution.py:366
